TPU v7x, 32 devices: a whole 2x2x4 slice. The times are simulated.
32 devices in a mesh: rep: 4 (over y, x), ctx: 8 (over z, core).
Axes of the slice: x: 2, y: 2, z: 4, core: 2. Of those that a mesh axis runs over, the one named last changes fastest.
Arguments:
- tokens: bfloat16 [4, 1024, 1024], P('rep', 'ctx'), may hold values from -6 to 6
- segment_ids: int32 [4, 1024], P('rep'), may hold values from 0 to 3, as said below
- positions: int32 [4, 1024], P('rep'), may hold values from 0 to 767, as said below
- cotangent: bfloat16 [4, 1024, 1024], P('rep', 'ctx'), may hold values from -6 to 6
- qkv_weight: bfloat16 [2, 1024, 4096], P(None, 'ctx'), may hold values from -0.1875 to 0.1875
- out_weight: bfloat16 [2, 2048, 1024], P(None, 'ctx'), may hold values from -0.5 to 0.5
- attn_gain: bfloat16 [2, 1024], P(None, 'ctx'), may hold values from 0.3984375 to 1.59375
- query_gain: bfloat16 [2, 128], P(None, 'ctx'), may hold values from 0.25 to 1.75
- key_gain: bfloat16 [2, 128], P(None, 'ctx'), may hold values from 0.25 to 1.75
- mlp_gain: bfloat16 [2, 1024], P(None, 'ctx'), may hold values from 0.3984375 to 1.59375
- gate_up_weight: bfloat16 [2, 1024, 6144], P(None, 'ctx'), may hold values from -0.1875 to 0.1875
- down_weight: bfloat16 [2, 3072, 1024], P(None, 'ctx'), may hold values from -0.21875 to 0.21875
Outputs:
- outputs: bfloat16 [4, 1024, 1024], P('rep', 'ctx')
- input_grad: float32 [4, 1024, 1024], P('rep', 'ctx')
- qkv_grad: float32 [2, 1024, 4096], P(None, 'ctx')
- out_grad: float32 [2, 2048, 1024], P(None, 'ctx')
- attn_gain_grad: float32 [2, 1024], P(None, 'ctx')
- query_gain_grad: float32 [2, 128], P(None, 'ctx')
- key_gain_grad: float32 [2, 128], P(None, 'ctx')
- mlp_gain_grad: float32 [2, 1024], P(None, 'ctx')
- gate_up_grad: float32 [2, 1024, 6144], P(None, 'ctx')
- down_grad: float32 [2, 3072, 1024], P(None, 'ctx')
Inputs may be any that keep to these rules, and one draw needn't show every extreme that they name: `segment_ids`: each sequence packs four documents with ids 0, 1, 2, 3 in order, never falling; one document, the first or the last, has exactly 768 tokens. `positions`: the index of a token within its document: 0 at a document's first token, rising by one along it.
All inputs are finite; a program needn't handle non-finite values.
Results may differ from a plain program's by a relative error of at most 0.025.
Values may be sent and summed in bfloat16 or wider, within the bound.
No kernel may reach another device: no remote copies, remote signals or barrier semaphores. Data moves between devices by JAX's collectives and lax.ppermute only.
A program may use at most 384 MiB of HBM per device.

v0:
```python
from functools import partial

import jax
import jax.numpy as jnp
from jax import lax
from jax.sharding import PartitionSpec as P

QUERY_HEADS = 16
KEY_VALUE_HEADS = 8
HEAD_SIZE = 128


EPS = 1e-06
THETA = 1000000.0


def as_sent(array):
    return jax.tree.map(lambda a: a.astype(jnp.bfloat16) if a.dtype == jnp.float32 else a, array)


def root_mean_square_norm(inputs, scale_gain):
    return inputs * lax.rsqrt(jnp.mean(inputs * inputs, axis=-1, keepdims=True) + EPS) * scale_gain


def rotary_apply(inputs, cosine_table, sine_table):
    half_width = inputs.shape[-1] // 2
    turned = jnp.concatenate([-inputs[..., half_width:], inputs[..., :half_width]], axis=-1)
    return inputs * cosine_table + turned * sine_table


def phases(token_pos, width):
    frequency = THETA ** (-(jnp.arange(width // 2).astype(jnp.float32) * 2.0) / width)
    angle = token_pos.astype(jnp.float32)[:, None] * frequency[None, :]
    angle = jnp.concatenate([angle, angle], axis=-1)
    return (jnp.cos(angle)[:, None, :], jnp.sin(angle)[:, None, :])


def contract_rows(left, right):
    return lax.dot_general(
        left, right, (((0,), (0,)), ((), ())), preferred_element_type=jnp.float32
    )


def contract_cols(left, right):
    return lax.dot_general(
        left, right, (((1,), (1,)), ((), ())), preferred_element_type=jnp.float32
    )


def swiglu(gate_up):
    width = gate_up.shape[1] // 2
    return jax.nn.silu(gate_up[:, :width]) * gate_up[:, width:]


def head_states(projected_rows, gain_q, key_gain_vector, cosine_table, sine_table):
    total_count = projected_rows.shape[0]
    query_matrix = root_mean_square_norm(
        projected_rows[:, : QUERY_HEADS * HEAD_SIZE].reshape(total_count, QUERY_HEADS, HEAD_SIZE),
        gain_q,
    )
    rows_of_keys = root_mean_square_norm(
        projected_rows[
            :, QUERY_HEADS * HEAD_SIZE : (QUERY_HEADS + KEY_VALUE_HEADS) * HEAD_SIZE
        ].reshape(total_count, KEY_VALUE_HEADS, HEAD_SIZE),
        key_gain_vector,
    )
    return (
        rotary_apply(query_matrix, cosine_table, sine_table),
        rotary_apply(rows_of_keys, cosine_table, sine_table),
    )


def score_block(query_head, key_head, allowed):
    raw_scores = jnp.einsum("tgd,sd->gts", query_head, key_head, preferred_element_type=jnp.float32)
    return jnp.where(allowed, raw_scores * HEAD_SIZE ** (-0.5), -1e30)


def head_forward(allowed, pieces):
    query_head, key_head, value_head = pieces
    scores = score_block(query_head, key_head, allowed)
    row_max = jnp.max(scores, axis=-1, keepdims=True)
    expo_vals = jnp.exp(scores - row_max)
    norm_sum = jnp.sum(expo_vals, axis=-1, keepdims=True)
    probs_b = (expo_vals / norm_sum).astype(jnp.bfloat16)
    attn_out = jnp.einsum("gts,sd->tgd", probs_b, value_head, preferred_element_type=jnp.float32)
    return (attn_out, row_max + jnp.log(norm_sum))


def grad_block(query_head, key_head, value_head, dout_head, total_head, offset_head, allowed):
    probability = jnp.exp(score_block(query_head, key_head, allowed) - total_head)
    d_probs = jnp.einsum("tgd,sd->gts", dout_head, value_head, preferred_element_type=jnp.float32)
    offset_head = jnp.sum(probability * d_probs, axis=-1, keepdims=True)
    d_scores_b = (probability * (d_probs - offset_head)).astype(jnp.bfloat16)
    return (probability, d_scores_b, offset_head)


def both_sides(allowed, pieces):
    query_head, key_head, value_head, dout_head, total_head = pieces
    probability, d_scores_b, offset_head = grad_block(
        query_head, key_head, value_head, dout_head, total_head, None, allowed
    )
    d_query = jnp.einsum(
        "gts,sd->tgd", d_scores_b, key_head, preferred_element_type=jnp.float32
    ) * HEAD_SIZE ** (-0.5)
    d_key = jnp.einsum(
        "gts,tgd->sd", d_scores_b, query_head, preferred_element_type=jnp.float32
    ) * HEAD_SIZE ** (-0.5)
    d_value = jnp.einsum(
        "gts,tgd->sd",
        probability.astype(jnp.bfloat16),
        dout_head,
        preferred_element_type=jnp.float32,
    )
    return (d_query, d_key, d_value)


def head_major(rows_matrix, total_count):
    return rows_matrix.reshape(
        total_count, KEY_VALUE_HEADS, QUERY_HEADS // KEY_VALUE_HEADS, HEAD_SIZE
    ).transpose(1, 0, 2, 3)


def kv_major(rows_matrix, total_count):
    return rows_matrix.reshape(total_count, KEY_VALUE_HEADS, HEAD_SIZE).transpose(1, 0, 2)


def stats_major(softmax_statistics, total_count):
    return softmax_statistics.T.reshape(
        KEY_VALUE_HEADS, QUERY_HEADS // KEY_VALUE_HEADS, total_count, 1
    )


def column_product(left, right):
    return contract_rows(left, right)


def local(
    tokens,
    segment_ids,
    positions,
    cotangent,
    qkv_weight,
    out_weight,
    attn_gain,
    query_gain,
    key_gain,
    mlp_gain,
    gate_up_weight,
    down_weight,
):
    count_of_rows = tokens.shape[1]
    count_of_keys = segment_ids.shape[1]
    layers = qkv_weight.shape[0]
    first_row = lax.axis_index("ctx") * count_of_rows
    my_rows = first_row + jnp.arange(count_of_rows, dtype=jnp.int32)
    all_rows = jnp.arange(count_of_keys, dtype=jnp.int32)
    seg_all = segment_ids[0]
    seg_mine = lax.dynamic_slice_in_dim(seg_all, first_row, count_of_rows)
    pos_mine = lax.dynamic_slice_in_dim(positions[0], first_row, count_of_rows)
    allowed = (seg_mine[:, None] == seg_all[None, :]) & (my_rows[:, None] >= all_rows[None, :])
    cosine_table, sine_table = phases(pos_mine, HEAD_SIZE)
    f32 = jnp.float32
    brain_float16 = jnp.bfloat16
    stream = tokens[0].astype(f32)
    saved = []
    for which_layer in range(layers):
        attn_set = (
            lax.all_gather(qkv_weight[which_layer], "ctx", axis=0, tiled=True),
            lax.all_gather(out_weight[which_layer], "ctx", axis=0, tiled=True),
            lax.all_gather(attn_gain[which_layer], "ctx", axis=0, tiled=True),
            lax.all_gather(query_gain[which_layer], "ctx", axis=0, tiled=True),
            lax.all_gather(key_gain[which_layer], "ctx", axis=0, tiled=True),
        )
        w_qkv, w_out, gain_a, gain_q, key_gain_vector = attn_set
        normed = root_mean_square_norm(stream, gain_a.astype(f32)).astype(brain_float16)
        projected_rows = jnp.dot(normed, w_qkv, preferred_element_type=f32)
        query_matrix, rows_of_keys = head_states(
            projected_rows,
            gain_q.astype(f32),
            key_gain_vector.astype(f32),
            cosine_table,
            sine_table,
        )
        query_b = query_matrix.reshape(count_of_rows, QUERY_HEADS * HEAD_SIZE).astype(brain_float16)
        keys_brain_float = rows_of_keys.reshape(count_of_rows, KEY_VALUE_HEADS * HEAD_SIZE).astype(
            brain_float16
        )
        values_brain_float = projected_rows[
            :, (QUERY_HEADS + KEY_VALUE_HEADS) * HEAD_SIZE :
        ].astype(brain_float16)
        keys_all, values_all = (
            lax.all_gather(keys_brain_float, "ctx", axis=0, tiled=True),
            lax.all_gather(values_brain_float, "ctx", axis=0, tiled=True),
        )
        attn_heads, total_heads = lax.map(
            partial(head_forward, allowed),
            (
                head_major(query_b, count_of_rows),
                kv_major(keys_all, count_of_keys),
                kv_major(values_all, count_of_keys),
            ),
        )
        attended = (
            attn_heads.transpose(1, 0, 2, 3)
            .reshape(count_of_rows, QUERY_HEADS * HEAD_SIZE)
            .astype(brain_float16)
        )
        log_total = total_heads.reshape(QUERY_HEADS, count_of_rows).T
        middle = stream + jnp.dot(attended, w_out, preferred_element_type=f32)
        mlp_set = (
            lax.all_gather(gate_up_weight[which_layer], "ctx", axis=0, tiled=True),
            lax.all_gather(down_weight[which_layer], "ctx", axis=0, tiled=True),
            lax.all_gather(mlp_gain[which_layer], "ctx", axis=0, tiled=True),
        )
        w_gu, w_down, gain_m = mlp_set
        normed_mid = root_mean_square_norm(middle, gain_m.astype(f32)).astype(brain_float16)
        gate_up = jnp.dot(normed_mid, w_gu, preferred_element_type=f32)
        hidden_b = swiglu(gate_up).astype(brain_float16)
        saved.append(
            (
                stream,
                normed,
                projected_rows,
                query_b,
                keys_all,
                values_all,
                log_total,
                attended,
                middle,
                normed_mid,
                gate_up,
                hidden_b,
            )
        )
        stream = middle + jnp.dot(hidden_b, w_down, preferred_element_type=f32)
    upstream = cotangent[0].astype(f32)
    results = [None] * layers
    for which_layer in reversed(range(layers)):
        (
            stream_in,
            normed,
            projected_rows,
            query_b,
            keys_all,
            values_all,
            log_total,
            attended,
            middle,
            normed_mid,
            gate_up,
            hidden_b,
        ) = saved[which_layer]
        w_gu, w_down, gain_m = (
            lax.all_gather(gate_up_weight[which_layer], "ctx", axis=0, tiled=True),
            lax.all_gather(down_weight[which_layer], "ctx", axis=0, tiled=True),
            lax.all_gather(mlp_gain[which_layer], "ctx", axis=0, tiled=True),
        )
        branch_b = upstream.astype(brain_float16)
        d_hidden = contract_cols(branch_b, w_down)
        swiglu_out, backward_function = jax.vjp(swiglu, gate_up)
        d_gate_up_b = backward_function(d_hidden)[0].astype(brain_float16)
        down_part = lax.psum_scatter(
            column_product(hidden_b, branch_b).astype(jnp.bfloat16),
            "ctx",
            scatter_dimension=0,
            tiled=True,
        ).astype(jnp.float32)
        gate_up_part = lax.psum_scatter(
            column_product(normed_mid, d_gate_up_b).astype(jnp.bfloat16),
            "ctx",
            scatter_dimension=0,
            tiled=True,
        ).astype(jnp.float32)
        d_normed_mid = contract_cols(d_gate_up_b, w_gu)
        norm_out, backward_function = jax.vjp(root_mean_square_norm, middle, gain_m.astype(f32))
        d_middle, d_gain_m = backward_function(d_normed_mid)
        d_middle = d_middle + upstream
        w_qkv, w_out, gain_a, gain_q, key_gain_vector = (
            lax.all_gather(qkv_weight[which_layer], "ctx", axis=0, tiled=True),
            lax.all_gather(out_weight[which_layer], "ctx", axis=0, tiled=True),
            lax.all_gather(attn_gain[which_layer], "ctx", axis=0, tiled=True),
            lax.all_gather(query_gain[which_layer], "ctx", axis=0, tiled=True),
            lax.all_gather(key_gain[which_layer], "ctx", axis=0, tiled=True),
        )
        out_branch = d_middle.astype(brain_float16)
        d_attended_b = contract_cols(out_branch, w_out).astype(brain_float16)
        d_w_out = contract_rows(attended, out_branch)
        query_heads = head_major(query_b, count_of_rows)
        dout_heads = head_major(d_attended_b, count_of_rows)
        key_heads = kv_major(keys_all, count_of_keys)
        value_heads = kv_major(values_all, count_of_keys)
        total_heads = stats_major(log_total, count_of_rows)
        d_query_heads, key_heads_gradient, value_heads_gradient = lax.map(
            partial(both_sides, allowed),
            (query_heads, key_heads, value_heads, dout_heads, total_heads),
        )
        all_keys_gradient = key_heads_gradient.transpose(1, 0, 2).reshape(
            count_of_keys, KEY_VALUE_HEADS * HEAD_SIZE
        )
        all_values_gradient = value_heads_gradient.transpose(1, 0, 2).reshape(
            count_of_keys, KEY_VALUE_HEADS * HEAD_SIZE
        )
        keys_gradient, values_gradient = (
            lax.psum_scatter(
                all_keys_gradient.astype(jnp.bfloat16), "ctx", scatter_dimension=0, tiled=True
            ).astype(jnp.float32),
            lax.psum_scatter(
                all_values_gradient.astype(jnp.bfloat16), "ctx", scatter_dimension=0, tiled=True
            ).astype(jnp.float32),
        )
        queries_gradient = d_query_heads.transpose(1, 0, 2, 3).reshape(
            count_of_rows, QUERY_HEADS, HEAD_SIZE
        )
        head_out, backward_function = jax.vjp(
            lambda proj_in, q_gain_in, k_gain_in: head_states(
                proj_in, q_gain_in, k_gain_in, cosine_table, sine_table
            ),
            projected_rows,
            gain_q.astype(f32),
            key_gain_vector.astype(f32),
        )
        projected_gradient, query_gain_gradient, key_gain_gradient = backward_function(
            (queries_gradient, keys_gradient.reshape(count_of_rows, KEY_VALUE_HEADS, HEAD_SIZE))
        )
        d_projected_b = jnp.concatenate(
            [projected_gradient[:, : (QUERY_HEADS + KEY_VALUE_HEADS) * HEAD_SIZE], values_gradient],
            axis=1,
        ).astype(brain_float16)
        d_w_qkv = contract_rows(normed, d_projected_b)
        d_normed = contract_cols(d_projected_b, w_qkv)
        norm_out, backward_function = jax.vjp(root_mean_square_norm, stream_in, gain_a.astype(f32))
        d_stream, d_gain_a = backward_function(d_normed)
        upstream = d_stream + d_middle
        reduced = (
            lax.psum_scatter(
                d_w_qkv.astype(jnp.bfloat16), "ctx", scatter_dimension=0, tiled=True
            ).astype(jnp.float32),
            lax.psum_scatter(
                d_w_out.astype(jnp.bfloat16), "ctx", scatter_dimension=0, tiled=True
            ).astype(jnp.float32),
            lax.psum_scatter(
                d_gain_a.astype(jnp.bfloat16), "ctx", scatter_dimension=0, tiled=True
            ).astype(jnp.float32),
            lax.psum_scatter(
                query_gain_gradient.astype(jnp.bfloat16), "ctx", scatter_dimension=0, tiled=True
            ).astype(jnp.float32),
            lax.psum_scatter(
                key_gain_gradient.astype(jnp.bfloat16), "ctx", scatter_dimension=0, tiled=True
            ).astype(jnp.float32),
            lax.psum_scatter(
                d_gain_m.astype(jnp.bfloat16), "ctx", scatter_dimension=0, tiled=True
            ).astype(jnp.float32),
        )
        layer_grads = tuple(reduced) + (gate_up_part, down_part)
        results[which_layer] = layer_grads
    flat = tuple((member for group in results for member in group))
    summed = jax.tree.map(lambda part: part.astype(jnp.float32), lax.psum(as_sent(flat), "rep"))
    results = [
        tuple(summed[8 * which_layer : 8 * which_layer + 8]) for which_layer in range(layers)
    ]
    stacked = [
        jnp.stack([results[which_layer][member] for which_layer in range(layers)])
        for member in range(8)
    ]
    return (
        stream.astype(brain_float16)[None],
        upstream[None],
        stacked[0],
        stacked[1],
        stacked[2],
        stacked[3],
        stacked[4],
        stacked[5],
        stacked[6],
        stacked[7],
    )


def solution(mesh):
    return jax.shard_map(
        local,
        mesh=mesh,
        in_specs=(
            P("rep", "ctx", None),
            P("rep", None),
            P("rep", None),
            P("rep", "ctx", None),
            P(None, "ctx", None),
            P(None, "ctx", None),
            P(None, "ctx"),
            P(None, "ctx"),
            P(None, "ctx"),
            P(None, "ctx"),
            P(None, "ctx", None),
            P(None, "ctx", None),
        ),
        out_specs=(
            P("rep", "ctx", None),
            P("rep", "ctx", None),
            P(None, "ctx", None),
            P(None, "ctx", None),
            P(None, "ctx"),
            P(None, "ctx"),
            P(None, "ctx"),
            P(None, "ctx"),
            P(None, "ctx", None),
            P(None, "ctx", None),
        ),
        check_vma=False,
    )
```

profile of v0, /device:TPU:0, one launch (start us, length us, event | category | flops | bytes accessed | tf_op | source)
XLA Modules:
  0.0 1996.3 jit_solution(6761443263539635525)
XLA Ops:
  7.2 3.1 fusion.218
  10.5 13.5 all-gather
  24.1 71.2 %all-gather.37.cloned.1.call-done = bf16[1,1024,4096]{2,1,0:T(8,128)(2,1)} async-done(((bf16[1,128,4096]{2,1,0:T(8,128)(2,1)}), bf16[1,1024,4096]{2,1,0:T(8,128)(2,1)}) %all-gather.37.cloned.1.call-update) | async-done | bytes 8388624 | tf_op jit(solution)/shard_map/all_gather | solution.py:168
  95.3 4.7 fusion.114
  103.1 15.3 all-reduce.29
  126.9 3.9 fusion.217
  136.7 8.6 all-gather.5
  145.3 10.9 all-gather.8
  176.1 23.2 %while.56 = (s32[]{:T(128)}, bf16[8,128,2,128]{1,3,2,0:T(8,128)(2,1)S(1)}, f32[8,2,128,1]{2,1,3,0:T(2,128)S(1)}, bf16[8,1024,128]{1,2,0:T(8,128)(2,1)}, bf16[8,1...) while((s32[]{:T(128)}, ...), condition=%wide.region_6.7_spmd.clone, body=%wide.region_3.6_spmd.clone.sunk | while | flops 136707840 | bytes 4144233 | solution.py:195
  199.4 8.0 all-gather.39.cloned.1.call-done
  210.4 114.5 %all-gather.41.cloned.1.call-done = bf16[1,1024,6144]{2,1,0:T(8,128)(2,1)} async-done(((bf16[1,128,6144]{2,1,0:T(8,128)(2,1)}), bf16[1,1024,6144]{2,1,0:T(8,128)(2,1)}) %all-gather.41.cloned.1.call-update) | async-done | bytes 12582928 | tf_op jit(solution)/shard_map/all_gather | solution.py:211
  325.0 6.4 fusion.106
  333.5 55.8 %all-gather.43.cloned.1.call-done = bf16[1,3072,1024]{2,1,0:T(8,128)(2,1)} async-done(((bf16[1,384,1024]{2,1,0:T(8,128)(2,1)}), bf16[1,3072,1024]{2,1,0:T(8,128)(2,1)}) %all-gather.43.cloned.1.call-update) | async-done | bytes 6291472 | tf_op jit(solution)/shard_map/all_gather | solution.py:212
  389.4 3.9 multiply_reduce_fusion.20
  393.3 78.4 %all-gather.45.cloned.1.call-done = bf16[1,1024,4096]{2,1,0:T(8,128)(2,1)} async-done(((bf16[1,128,4096]{2,1,0:T(8,128)(2,1)}), bf16[1,1024,4096]{2,1,0:T(8,128)(2,1)}) %all-gather.45.cloned.1.call-update) | async-done | bytes 8388624 | tf_op jit(solution)/shard_map/all_gather | solution.py:168
  471.7 4.7 fusion.110
  486.4 9.3 all-gather.13
  502.4 4.0 all-gather.33.cloned.1.call-done
  506.3 3.5 copy.265
  509.9 4.1 copy.161
  514.0 23.1 %all-gather.35.cloned.1.call-done = bf16[1024,1024]{1,0:T(8,128)(2,1)} async-done(((bf16[128,1024]{1,0:T(8,128)(2,1)}), bf16[1024,1024]{1,0:T(8,128)(2,1)}) %all-gather.35.cloned.1.call-update) | async-done | bytes 2097168 | tf_op jit(solution)/shard_map/all_gather | solution.py:192
  537.1 3.3 bitcast_bitcast_fusion.2
  540.4 24.2 %while.57 = (s32[]{:T(128)}, bf16[8,128,2,128]{1,3,2,0:T(8,128)(2,1)S(1)}, f32[8,2,128,1]{2,1,3,0:T(2,128)S(1)}, bf16[8,1024,128]{1,2,0:T(8,128)(2,1)}, bf16[8,1...) while((s32[]{:T(128)}, ...), condition=%wide.region_14.15_spmd.clone, body=%wide.region_11.14_spmd.clone.sunk | while | flops 136707840 | bytes 4144233 | solution.py:195
  564.6 20.2 %all-gather.47.cloned.1.call-done = bf16[1,2048,1024]{2,1,0:T(8,128)(2,1)} async-done(((bf16[1,256,1024]{2,1,0:T(8,128)(2,1)}), bf16[1,2048,1024]{2,1,0:T(8,128)(2,1)}) %all-gather.47.cloned.1.call-update) | async-done | bytes 4194320 | tf_op jit(solution)/shard_map/all_gather | solution.py:169
  584.8 3.0 multiply_reduce_fusion.18
  587.9 114.7 %all-gather.49.cloned.1.call-done = bf16[1,1024,6144]{2,1,0:T(8,128)(2,1)} async-done(((bf16[1,128,6144]{2,1,0:T(8,128)(2,1)}), bf16[1,1024,6144]{2,1,0:T(8,128)(2,1)}) %all-gather.49.cloned.1.call-update) | async-done | bytes 12582928 | tf_op jit(solution)/shard_map/all_gather | solution.py:211
  702.6 8.1 fusion.102
  710.7 56.3 %all-gather.51.cloned.1.call-done = bf16[1,3072,1024]{2,1,0:T(8,128)(2,1)} async-done(((bf16[1,384,1024]{2,1,0:T(8,128)(2,1)}), bf16[1,3072,1024]{2,1,0:T(8,128)(2,1)}) %all-gather.51.cloned.1.call-update) | async-done | bytes 6291472 | tf_op jit(solution)/shard_map/all_gather | solution.py:212
  767.0 7.1 fusion.188
  774.2 10.8 multiply_reduce_fusion.8
  788.0 3.3 bitcast_bitcast_fusion
  795.6 72.2 %while.58 = (s32[]{:T(128)}, f32[8,128,2,128]{1,3,2,0:T(8,128)}, bf16[8,1024,128]{1,2,0:T(8,128)(2,1)}, bf16[8,1024,128]{1,2,0:T(8,128)(2,1)}, bf16[8,1024,128]{...) while((s32[]{:T(128)}, f32[8,128,2,128]{1,3,2,0:T(8,128)}, ...), condition=%wide.region_19.20_spmd.clone, body=%wide.region_17.19_spmd.clone.sunk | while | flops 338591488 | bytes 15350969 | solution.py:293
  867.8 4.0 copy.196
  884.3 22.3 %reduce-scatter.37.cloned.1.call-done = bf16[128,1024]{1,0:T(8,128)(2,1)} async-done(((bf16[1024,1024]{1,0:T(8,128)(2,1)}), bf16[128,1024]{1,0:T(8,128)(2,1)}) %reduce-scatter.37.cloned.1.call-update) | async-done | bytes 262160
  910.6 33.3 %reduce-scatter.39.cloned.1.call-done = bf16[128,1024]{1,0:T(8,128)(2,1)} async-done(((bf16[1024,1024]{1,0:T(8,128)(2,1)}), bf16[128,1024]{1,0:T(8,128)(2,1)}) %reduce-scatter.39.cloned.1.call-update) | async-done | bytes 262160 | tf_op jit(solution)/shard_map/reduce_scatter | solution.py:307
  944.0 7.1 multiply_reduce_fusion.12
  951.4 5.5 fusion.187
  956.9 10.7 multiply_reduce_fusion.9
  975.8 75.6 %while.59 = (s32[]{:T(128)}, f32[8,128,2,128]{1,3,2,0:T(8,128)}, bf16[8,1024,128]{1,2,0:T(8,128)(2,1)}, bf16[8,1024,128]{1,2,0:T(8,128)(2,1)}, bf16[8,1024,128]{...) while((s32[]{:T(128)}, f32[8,128,2,128]{1,3,2,0:T(8,128)}, ...), condition=%wide.region_28.29_spmd.clone, body=%wide.region_26.28_spmd.clone.sunk | while | flops 338591488 | bytes 11156609 | solution.py:293
  1051.3 3.9 copy.200
  1060.7 3.3 convolution_convert_fusion.6
  1065.1 3.2 convolution_convert_fusion.7
  1069.6 4.5 convolution_convert_fusion.4
  1075.4 4.5 convolution_convert_fusion.5
  1081.1 5.7 convolution_convert_fusion.2
  1101.3 25.9 %reduce-scatter.43.cloned.1.call-done = bf16[128,1024]{1,0:T(8,128)(2,1)} async-done(((bf16[1024,1024]{1,0:T(8,128)(2,1)}), bf16[128,1024]{1,0:T(8,128)(2,1)}) %reduce-scatter.43.cloned.1.call-update) | async-done | bytes 262160 | tf_op jit(solution)/shard_map/reduce_scatter | solution.py:307
  1127.2 6.9 convolution_convert_fusion.3
  1135.3 8.5 convolution_convert_fusion
  1144.4 8.5 convolution_convert_fusion.1
  1153.2 25.5 %reduce-scatter.27.cloned.1.call-done = bf16[256,1024]{1,0:T(8,128)(2,1)} async-done(((bf16[2048,1024]{1,0:T(8,128)(2,1)}), bf16[256,1024]{1,0:T(8,128)(2,1)}) %reduce-scatter.27.cloned.1.call-update) | async-done | bytes 524304 | tf_op jit(solution)/shard_map/reduce_scatter | solution.py:338
  1178.6 50.6 %reduce-scatter.25.cloned.1.call-done = bf16[256,1024]{1,0:T(8,128)(2,1)} async-done(((bf16[2048,1024]{1,0:T(8,128)(2,1)}), bf16[256,1024]{1,0:T(8,128)(2,1)}) %reduce-scatter.25.cloned.1.call-update) | async-done | bytes 524304 | tf_op jit(solution)/shard_map/reduce_scatter | solution.py:338
  1229.2 71.1 %reduce-scatter.35.cloned.1.call-done = bf16[384,1024]{1,0:T(8,128)(2,1)} async-done(((bf16[3072,1024]{1,0:T(8,128)(2,1)}), bf16[384,1024]{1,0:T(8,128)(2,1)}) %reduce-scatter.35.cloned.1.call-update) | async-done | bytes 786448 | tf_op jit(solution)/shard_map/reduce_scatter | solution.py:262
  1300.4 70.4 %reduce-scatter.33.cloned.1.call-done = bf16[384,1024]{1,0:T(8,128)(2,1)} async-done(((bf16[3072,1024]{1,0:T(8,128)(2,1)}), bf16[384,1024]{1,0:T(8,128)(2,1)}) %reduce-scatter.33.cloned.1.call-update) | async-done | bytes 786448 | tf_op jit(solution)/shard_map/reduce_scatter | solution.py:262
  1370.7 90.3 %reduce-scatter.23.cloned.1.call-done = bf16[128,4096]{1,0:T(8,128)(2,1)} async-done(((bf16[1024,4096]{1,0:T(8,128)(2,1)}), bf16[128,4096]{1,0:T(8,128)(2,1)}) %reduce-scatter.23.cloned.1.call-update) | async-done | bytes 1048592 | tf_op jit(solution)/shard_map/reduce_scatter | solution.py:335
  1461.0 90.3 %reduce-scatter.21.cloned.1.call-done = bf16[128,4096]{1,0:T(8,128)(2,1)} async-done(((bf16[1024,4096]{1,0:T(8,128)(2,1)}), bf16[128,4096]{1,0:T(8,128)(2,1)}) %reduce-scatter.21.cloned.1.call-update) | async-done | bytes 1048592 | tf_op jit(solution)/shard_map/reduce_scatter | solution.py:335
  1551.4 129.9 %reduce-scatter.31.cloned.1.call-done = bf16[128,6144]{1,0:T(8,128)(2,1)} async-done(((bf16[1024,6144]{1,0:T(8,128)(2,1)}), bf16[128,6144]{1,0:T(8,128)(2,1)}) %reduce-scatter.31.cloned.1.call-update) | async-done | bytes 1572880 | tf_op jit(solution)/shard_map/reduce_scatter | solution.py:268
  1681.3 129.8 %reduce-scatter.29.cloned.1.call-done = bf16[128,6144]{1,0:T(8,128)(2,1)} async-done(((bf16[1024,6144]{1,0:T(8,128)(2,1)}), bf16[128,6144]{1,0:T(8,128)(2,1)}) %reduce-scatter.29.cloned.1.call-update) | async-done | bytes 1572880 | tf_op jit(solution)/shard_map/reduce_scatter | solution.py:268
  1812.5 4.6 fusion.161
  1817.1 7.3 fusion.172
  1824.4 25.9 %all-reduce.28 = (bf16[1024]{0:T(1024)(128)(2,1)S(1)}, bf16[1024]{0:T(1024)(128)(2,1)S(1)}, bf16[128]{0:T(256)(128)(2,1)S(1)}, bf16[128]{0:T(256)(128)(2,1)S(1)}...) all-reduce(bf16[1024]{0:T(1024)(128)(2,1)S(1)} %copy-done.107, ...), channel_id=27, replica_groups=mesh['rep'=4,'ctx'=8] {'ctx'}, use_global_device_ids=true, to_apply=%region_46.47.clone | all-reduce | flops 4608 | bytes 18432
  1850.7 10.0 all-reduce.30
  1863.9 114.6 %all-reduce.34.cloned.1.call-done = (bf16[1,128,4096]{2,1,0:T(8,128)(2,1)}, bf16[1,128,4096]{2,1,0:T(8,128)(2,1)}, bf16[1,256,1024]{2,1,0:T(8,128)(2,1)}, bf16[1...) async-done(((bf16[1,128,4096]{2,1,0:T(8,128)(2,1)}, ...) | async-done | bytes 7864336 | tf_op jit(solution)/shard_map/psum | solution.py:357
  1978.5 3.4 maximum_convert_fusion.2
  1981.9 3.1 maximum_convert_fusion
  (747 shorter events, 318.0 us)
Async XLA Ops:
  7.2 16.7 copy-start.27
  7.2 88.1 %all-gather.37.cloned.1.call-start = ((), (), s32[]{:S(2)}) async-start(), calls=%async_computation.24 | async-start | bytes 9437184 | tf_op jit(solution)/shard_map/all_gather | solution.py:168
  10.4 158.5 %all-gather.29.cloned.1.call-start = ((), (), s32[]{:S(2)}) async-start(), calls=%async_computation.12 | async-start | bytes 2359296 | tf_op jit(solution)/shard_map/all_gather | solution.py:193
  23.9 76.1 %copy-start.73 = (f32[1,1024]{1,0:T(1,128)}, f32[1,1024]{1,0:T(1,128)S(1)}, u32[]{:S(2)}) copy-start(f32[1,1024]{1,0:T(1,128)S(1)} %convert_element_type.356) | copy-start | bytes 12292
  24.1 76.0 %copy-start.118 = (f32[128]{0:T(128)}, f32[128]{0:T(128)S(1)}, u32[]{:S(2)}) copy-start(f32[128]{0:T(128)S(1)} %fusion.178) | copy-start | bytes 1540
  24.1 76.0 %copy-start.99 = (f32[128]{0:T(128)}, f32[128]{0:T(128)S(1)}, u32[]{:S(2)}) copy-start(f32[128]{0:T(128)S(1)} %fusion.203) | copy-start | bytes 1540
  100.8 73.2 %all-gather.31.cloned.1.call-start = ((), (), s32[]{:S(2)}) async-start(), calls=%async_computation.13 | async-start | bytes 2359296 | tf_op jit(solution)/shard_map/all_gather | solution.py:192
  124.6 82.8 %all-gather.39.cloned.1.call-start = ((), (), s32[]{:S(2)}) async-start(), calls=%async_computation.25 | async-start | bytes 4718592 | tf_op jit(solution)/shard_map/all_gather | solution.py:169
  126.9 198.1 %all-gather.41.cloned.1.call-start = ((), (), s32[]{:S(2)}) async-start(), calls=%async_computation.26 | async-start | bytes 14155776 | tf_op jit(solution)/shard_map/all_gather | solution.py:211
  130.9 258.5 %all-gather.43.cloned.1.call-start = ((), (), s32[]{:S(2)}) async-start(), calls=%async_computation.27 | async-start | bytes 7077888 | tf_op jit(solution)/shard_map/all_gather | solution.py:212
  133.6 22.6 %copy-start.62 = (s32[1,1024]{1,0:T(1,128)S(1)}, s32[1,1024]{1,0:T(1,128)}, u32[]{:S(2)}) copy-start(s32[1,1024]{1,0:T(1,128)} %param.21) | copy-start | bytes 12292
  133.6 338.1 %all-gather.45.cloned.1.call-start = ((), (), s32[]{:S(2)}) async-start(), calls=%async_computation.28 | async-start | bytes 9437184 | tf_op jit(solution)/shard_map/all_gather | solution.py:168
  134.4 372.0 %all-gather.33.cloned.1.call-start = ((), (), s32[]{:S(2)}) async-start(), calls=%async_computation.14 | async-start | bytes 2359296 | tf_op jit(solution)/shard_map/all_gather | solution.py:193
  135.3 21.5 %copy-start.108 = (f32[128]{0:T(128)}, f32[128]{0:T(128)S(1)}, u32[]{:S(2)}) copy-start(f32[128]{0:T(128)S(1)} %convert_element_type.365) | copy-start | bytes 1540
  199.3 11.0 copy-start.38
  199.3 11.0 copy-start.76
  199.4 11.0 copy-start.90
  210.4 121.0 %copy-start.120 = (f32[128]{0:T(128)}, f32[128]{0:T(128)S(1)}, u32[]{:S(2)}) copy-start(f32[128]{0:T(128)S(1)} %get-tuple-element.581) | copy-start | bytes 1540
  210.4 179.0 %copy-start.4 = (f32[128,1024]{1,0:T(8,128)}, f32[128,1024]{1,0:T(8,128)S(1)}, u32[]{:S(2)}) copy-start(f32[128,1024]{1,0:T(8,128)S(1)} %get-tuple-element.582) | copy-start | bytes 1572868
  210.4 121.0 %copy-start.93 = (f32[128]{0:T(128)}, f32[128]{0:T(128)S(1)}, u32[]{:S(2)}) copy-start(f32[128]{0:T(128)S(1)} %fusion.204) | copy-start | bytes 1540
  333.5 59.7 %copy-start.23 = (bf16[128,3072]{1,0:T(8,128)(2,1)}, bf16[128,3072]{1,0:T(8,128)(2,1)S(1)}, u32[]{:S(2)}) copy-start(bf16[128,3072]{1,0:T(8,128)(2,1)S(1)} %multiply_convert_fusion.3) | copy-start | bytes 2359300
  393.3 83.1 %copy-start.122 = (f32[128]{0:T(128)}, f32[128]{0:T(128)S(1)}, u32[]{:S(2)}) copy-start(f32[128]{0:T(128)S(1)} %get-tuple-element.583) | copy-start | bytes 1540
  393.3 191.6 %copy-start.2 = (f32[128,1024]{1,0:T(8,128)}, f32[128,1024]{1,0:T(8,128)S(1)}, u32[]{:S(2)}) copy-start(f32[128,1024]{1,0:T(8,128)S(1)} %get-tuple-element.584) | copy-start | bytes 1572868
  393.3 83.1 %copy-start.96 = (f32[128]{0:T(128)}, f32[128]{0:T(128)S(1)}, u32[]{:S(2)}) copy-start(f32[128]{0:T(128)S(1)} %fusion.205) | copy-start | bytes 1540
  478.5 58.6 %all-gather.35.cloned.1.call-start = ((), (), s32[]{:S(2)}) async-start(), calls=%async_computation.15 | async-start | bytes 2359296 | tf_op jit(solution)/shard_map/all_gather | solution.py:192
  484.5 100.4 %all-gather.47.cloned.1.call-start = ((), (), s32[]{:S(2)}) async-start(), calls=%async_computation.29 | async-start | bytes 4718592 | tf_op jit(solution)/shard_map/all_gather | solution.py:169
  485.0 217.5 %all-gather.49.cloned.1.call-start = ((), (), s32[]{:S(2)}) async-start(), calls=%async_computation.30 | async-start | bytes 14155776 | tf_op jit(solution)/shard_map/all_gather | solution.py:211
  485.8 281.2 %all-gather.51.cloned.1.call-start = ((), (), s32[]{:S(2)}) async-start(), calls=%async_computation.31 | async-start | bytes 7077888 | tf_op jit(solution)/shard_map/all_gather | solution.py:212
  486.4 420.2 %reduce-scatter.37.cloned.1.call-start = ((), (), s32[]{:S(2)}) async-start(), calls=%async_computation.32 | async-start | bytes 2359296
  514.0 26.4 %copy-start.20 = (bf16[8,128,2,128]{1,3,2,0:T(8,128)(2,1)S(1)}, bf16[8,128,2,128]{1,3,2,0:T(8,128)(2,1)}, u32[]{:S(2)}) copy-start(bf16[8,128,2,128]{1,3,2,0:T(8,128)(2,1)} %copy-done.19) | copy-start | bytes 1572868
  514.0 26.4 %copy-start.77 = (s32[128]{0:T(128)S(1)}, s32[128]{0:T(128)}, u32[]{:S(2)}) copy-start(s32[128]{0:T(128)} %copy-done.76) | copy-start | bytes 1540
  514.0 26.4 %copy-start.81 = (s32[128]{0:T(128)S(1)}, s32[128]{0:T(128)}, u32[]{:S(2)}) copy-start(s32[128]{0:T(128)} %dynamic-slice_bitcast_fusion.8) | copy-start | bytes 1540
  564.6 146.1 %copy-start.21 = (bf16[8,128,2,128]{1,3,2,0:T(8,128)(2,1)}, bf16[8,128,2,128]{1,3,2,0:T(8,128)(2,1)S(1)}, u32[]{:S(2)}) copy-start(bf16[8,128,2,128]{1,3,2,0:T(8,128)(2,1)S(1)} %get-tuple-element.195) | copy-start | bytes 1572868
  587.8 197.1 %copy-start.6 = (f32[128,1024]{1,0:T(8,128)}, f32[128,1024]{1,0:T(8,128)S(1)}, u32[]{:S(2)}) copy-start(f32[128,1024]{1,0:T(8,128)S(1)} %get-tuple-element.586) | copy-start | bytes 1572868
  587.9 197.1 %copy-start.91 = (f32[128]{0:T(128)}, f32[128]{0:T(128)S(1)}, u32[]{:S(2)}) copy-start(f32[128]{0:T(128)S(1)} %fusion.206) | copy-start | bytes 1540
  702.6 64.4 %copy-start.65 = (bf16[1,128,1024]{2,1,0:T(8,128)(2,1)S(1)}, bf16[1,128,1024]{2,1,0:T(8,128)(2,1)}, u32[]{:S(2)}) copy-start(bf16[1,128,1024]{2,1,0:T(8,128)(2,1)} %param.23) | copy-start | bytes 786436
  774.1 10.8 copy-start.42
  774.2 10.8 copy-start.43
  774.2 10.8 copy-start.66
  774.2 11.0 copy-start.14
  871.8 72.2 %reduce-scatter.39.cloned.1.call-start = ((), (), s32[]{:S(2)}) async-start(), calls=%async_computation.33 | async-start | bytes 2359296 | tf_op jit(solution)/shard_map/reduce_scatter | solution.py:307
  875.9 219.2 %reduce-scatter.41.cloned.1.call-start = ((), (), s32[]{:S(2)}) async-start(), calls=%async_computation.34 | async-start | bytes 2359296
  910.4 33.6 %copy-start.3 = (f32[128,1024]{1,0:T(8,128)S(1)}, f32[128,1024]{1,0:T(8,128)}, u32[]{:S(2)}) copy-start(f32[128,1024]{1,0:T(8,128)} %copy-done.2) | copy-start | bytes 1572868
  910.6 40.5 %copy-start.40 = (bf16[128,3072]{1,0:T(8,128)(2,1)}, bf16[128,3072]{1,0:T(8,128)(2,1)S(1)}, u32[]{:S(2)}) copy-start(bf16[128,3072]{1,0:T(8,128)(2,1)S(1)} %fusion.143) | copy-start | bytes 2359300
  910.6 40.5 %copy-start.123 = (f32[128]{0:T(128)S(1)}, f32[128]{0:T(128)}, u32[]{:S(2)}) copy-start(f32[128]{0:T(128)} %copy-done.122) | copy-start | bytes 1540
  910.6 40.5 %copy-start.32 = (f32[128,1024]{1,0:T(8,128)S(1)}, f32[128,1024]{1,0:T(8,128)}, u32[]{:S(2)}) copy-start(f32[128,1024]{1,0:T(8,128)} %copy-done.31) | copy-start | bytes 1572868
  910.6 40.5 %copy-start.97 = (f32[128]{0:T(128)S(1)}, f32[128]{0:T(128)}, u32[]{:S(2)}) copy-start(f32[128]{0:T(128)} %copy-done.96) | copy-start | bytes 1540
  951.3 16.3 copy-start.48
  956.8 10.8 copy-start.44
  956.9 11.8 copy-start.13
  1055.3 71.9 %reduce-scatter.43.cloned.1.call-start = ((), (), s32[]{:S(2)}) async-start(), calls=%async_computation.35 | async-start | bytes 2359296 | tf_op jit(solution)/shard_map/reduce_scatter | solution.py:307
  1059.5 119.2 %reduce-scatter.27.cloned.1.call-start = ((), (), s32[]{:S(2)}) async-start(), calls=%async_computation.19 | async-start | bytes 4718592 | tf_op jit(solution)/shard_map/reduce_scatter | solution.py:338
  1064.0 165.3 %reduce-scatter.25.cloned.1.call-start = ((), (), s32[]{:S(2)}) async-start(), calls=%async_computation.18 | async-start | bytes 4718592 | tf_op jit(solution)/shard_map/reduce_scatter | solution.py:338
  1068.4 231.9 %reduce-scatter.35.cloned.1.call-start = ((), (), s32[]{:S(2)}) async-start(), calls=%async_computation.23 | async-start | bytes 7077888 | tf_op jit(solution)/shard_map/reduce_scatter | solution.py:262
  1074.1 296.6 %reduce-scatter.33.cloned.1.call-start = ((), (), s32[]{:S(2)}) async-start(), calls=%async_computation.22 | async-start | bytes 7077888 | tf_op jit(solution)/shard_map/reduce_scatter | solution.py:262
  1080.0 381.1 %reduce-scatter.23.cloned.1.call-start = ((), (), s32[]{:S(2)}) async-start(), calls=%async_computation.17 | async-start | bytes 9437184 | tf_op jit(solution)/shard_map/reduce_scatter | solution.py:335
  1086.9 464.4 %reduce-scatter.21.cloned.1.call-start = ((), (), s32[]{:S(2)}) async-start(), calls=%async_computation.16 | async-start | bytes 9437184 | tf_op jit(solution)/shard_map/reduce_scatter | solution.py:335
  1100.2 27.0 %copy-start.28 = (bf16[1,128,1024]{2,1,0:T(8,128)(2,1)S(1)}, bf16[1,128,1024]{2,1,0:T(8,128)(2,1)}, u32[]{:S(2)}) copy-start(bf16[1,128,1024]{2,1,0:T(8,128)(2,1)} %param.20) | copy-start | bytes 786436
  1100.2 27.0 %copy-start.74 = (f32[1,1024]{1,0:T(1,128)S(1)}, f32[1,1024]{1,0:T(1,128)}, u32[]{:S(2)}) copy-start(f32[1,1024]{1,0:T(1,128)} %copy-done.73) | copy-start | bytes 12292
  1100.2 27.0 %copy-start.100 = (f32[128]{0:T(128)S(1)}, f32[128]{0:T(128)}, u32[]{:S(2)}) copy-start(f32[128]{0:T(128)} %copy-done.99) | copy-start | bytes 1540
  1134.2 547.1 %reduce-scatter.31.cloned.1.call-start = ((), (), s32[]{:S(2)}) async-start(), calls=%async_computation.21 | async-start | bytes 14155776 | tf_op jit(solution)/shard_map/reduce_scatter | solution.py:268
  1143.8 667.3 %reduce-scatter.29.cloned.1.call-start = ((), (), s32[]{:S(2)}) async-start(), calls=%async_computation.20 | async-start | bytes 14155776 | tf_op jit(solution)/shard_map/reduce_scatter | solution.py:268
  1152.9 825.6 %all-reduce.34.cloned.1.call-start = ((), (), s32[]{:S(2)}) async-start(), calls=%async_computation.36 | async-start | bytes 15728640 | tf_op jit(solution)/shard_map/psum | solution.py:357
  1817.1 45.8 %copy-start.119 = (f32[128]{0:T(128)S(1)}, f32[128]{0:T(128)}, u32[]{:S(2)}) copy-start(f32[128]{0:T(128)} %copy-done.118) | copy-start | bytes 1540
  (102 other events, 298.0 us)
Sparse Core Ops, SparseCore 0:
  10.5 84.7 all-gather.36
  101.0 27.8 all-gather.28
  130.5 28.5 all-gather.30
  161.1 46.2 all-gather.38
  209.4 115.5 all-gather.40
  326.5 62.8 all-gather.42
  391.0 80.6 all-gather.44
  478.6 27.6 all-gather.32
  508.5 28.5 all-gather.34
  538.5 46.2 all-gather.46
  587.0 115.4 all-gather.48
  704.1 62.8 all-gather.50
  871.9 34.6 reduce-scatter.36
  909.3 34.6 reduce-scatter.38
  1055.4 34.5 reduce-scatter.40
  1092.8 34.4 reduce-scatter.42
  1130.0 48.6 reduce-scatter.26
  1180.8 48.4 reduce-scatter.24
  1232.1 68.1 reduce-scatter.34
  1302.5 68.1 reduce-scatter.32
  1373.0 87.9 reduce-scatter.22
  1463.3 87.9 reduce-scatter.20
  1553.7 127.5 reduce-scatter.30
  1683.4 127.5 reduce-scatter.28
  1815.6 162.8 all-reduce.33
where the time goes:
time: 2010 us; the launch traced here: 2000 us
  waiting for transfers between devices  1400 us (70%)
  matrix products  298 us (15%)
  local copies, waits for them, and re-layouts  127 us (6%)
  blocking collectives  93.4 us (5%)
  other arithmetic  53.5 us (3%)
    reduce_scatter x2, waiting for transfers between devices, local(): lax.psum_scatter(column_product(normed_mid, d_gate_up_b).astype(jnp.bfloa...  260 us
    all_gather x2, waiting for transfers between devices, local(): lax.all_gather(gate_up_weight[which_layer], 'ctx', axis=0, tiled=True)  229 us
    reduce_scatter x2, waiting for transfers between devices, local(): lax.psum_scatter(d_w_qkv.astype(jnp.bfloat16), 'ctx', scatter_dimension=0...  181 us
    all_gather x2, waiting for transfers between devices, local(): lax.all_gather(qkv_weight[which_layer], 'ctx', axis=0, tiled=True)  150 us
    reduce_scatter x2, waiting for transfers between devices, local(): lax.psum_scatter(column_product(hidden_b, branch_b).astype(jnp.bfloat16),...  141 us
    psum x1, waiting for transfers between devices, local(): lax.psum(as_sent(flat), 'rep')  115 us
    all_gather x2, waiting for transfers between devices, local(): lax.all_gather(down_weight[which_layer], 'ctx', axis=0, tiled=True)  112 us
    reduce_scatter x2, waiting for transfers between devices, local(): lax.psum_scatter(d_w_out.astype(jnp.bfloat16), 'ctx', scatter_dimension=0...  76.1 us
  transfers between devices with their start and end apart: 25, of which 22 were waited for; matrix products, arithmetic and copies ran while one was open for 11% of the time, Pallas kernels for 0%

commit v1 on v0

v1 whole, which is shorter than its diff:
```python
from functools import partial

import jax
import jax.numpy as jnp
from jax import lax
from jax.experimental import pallas as pl
from jax.experimental.pallas import tpu as pltpu
from jax.sharding import PartitionSpec as P

QUERY_HEADS = 16
KEY_VALUE_HEADS = 8
GROUP = QUERY_HEADS // KEY_VALUE_HEADS
HEAD = 128
EPS = 1e-06
THETA = 1000000.0
SCALE = HEAD**-0.5
BF = jnp.bfloat16
F32 = jnp.float32
AXES = ("rep", "ctx")
VMEM_LIMIT = 56 * 1024 * 1024


def dot(a, b):
    return jnp.dot(a, b, preferred_element_type=F32)


def dot_rows(a, b):
    return lax.dot_general(a, b, (((0,), (0,)), ((), ())), preferred_element_type=F32)


def dot_cols(a, b):
    return lax.dot_general(a, b, (((1,), (1,)), ((), ())), preferred_element_type=F32)


class Moves:
    def __init__(self, reps, ctxs):
        self.reps, self.ctxs = reps, ctxs
        at = lambda r, z, c: r * ctxs + 2 * z + c
        every = [(r, z, c) for r in range(reps) for z in range(ctxs // 2) for c in range(2)]
        self.swap = [(at(r, z, c), at(z, r, c)) for r, z, c in every]
        self.other = [(at(r, z, c), at(r, z, 1 - c)) for r, z, c in every]
        self.peer = [[(at(r, z, c), at(r ^ d, z, c)) for r, z, c in every] for d in range(reps)]
        self.order = sorted(range(1, reps), key=lambda d: -bin(d).count("1"))

    def turn(self, value):
        return lax.ppermute(value, AXES, self.swap)

    def sibling(self, value):
        return lax.ppermute(value, AXES, self.other)

    def gather(self, value):
        pieces = [value] + [None] * (self.reps - 1)
        for d in self.order:
            pieces[d] = lax.ppermute(value, AXES, self.peer[d])
        return pieces

    def scatter(self, make):
        got = [lax.ppermute(make(d).astype(BF), AXES, self.peer[d]) for d in self.order]
        total = make(0)
        for term in got:
            total = total + term.astype(F32)
        return total


def whole(*shape):
    return pl.BlockSpec(shape, lambda *_: (0,) * len(shape))


def rotate(v, cosine, sine):
    return v * cosine + pltpu.roll(v, HEAD // 2, 1) * sine


def rotate_back(d, cosine, sine):
    return d * cosine + pltpu.roll(d * sine, HEAD // 2, 1)


def qkv_body(pieces, nq, nk, *refs):
    xs, (w, qg, kg, cs, sn, q_out, kv_out, proj_out, held) = refs[:pieces], refs[pieces:]
    t = xs[0].shape[0]
    for j in range(pieces):
        held[j * t : (j + 1) * t, :] = xs[j][...]
    x = held[...]
    cosine, sine = cs[...], sn[...]
    heads = nq + 2 * nk
    for h in range(0, heads, 2):
        wide = min(2, heads - h)
        y2 = dot(x, w[:, h * HEAD : (h + wide) * HEAD])
        for i in range(wide):
            y = y2[:, i * HEAD : (i + 1) * HEAD]
            n = h + i
            if n < nq + nk:
                proj_out[:, n * HEAD : (n + 1) * HEAD] = y
                gain = (qg if n < nq else kg)[...]
                y = y * lax.rsqrt(jnp.mean(y * y, axis=-1, keepdims=True) + EPS) * gain
                y = rotate(y, cosine, sine)
            if n < nq:
                q_out[:, n * HEAD : (n + 1) * HEAD] = y.astype(BF)
            else:
                kv_out[:, (n - nq) * HEAD : (n - nq + 1) * HEAD] = y.astype(BF)


def qkv_call(xs, w, qg, kg, cs, sn, nq, nk):
    t, d = xs[0].shape
    n = t * len(xs)
    return pl.pallas_call(
        partial(qkv_body, len(xs), nq, nk),
        out_shape=(
            jax.ShapeDtypeStruct((n, nq * HEAD), BF),
            jax.ShapeDtypeStruct((n, 2 * nk * HEAD), BF),
            jax.ShapeDtypeStruct((n, (nq + nk) * HEAD), F32),
        ),
        scratch_shapes=[pltpu.VMEM((n, d), BF)],
        compiler_params=pltpu.CompilerParams(vmem_limit_bytes=VMEM_LIMIT),
        cost_estimate=pl.CostEstimate(
            flops=2 * n * d * (nq + 2 * nk) * HEAD, transcendentals=0, bytes_accessed=8 << 20
        ),
        name="qkv",
    )(*xs, w, qg, kg, cs, sn)


def fill(place, own, sib, dst, reps, t):
    r, c = place[0], place[1]
    for kk in range(reps):
        blk = pl.multiple_of((kk ^ r) * t, t)
        dst[pl.ds(pl.multiple_of((2 * kk + c) * t, t), t), :] = own[pl.ds(blk, t), :]
        dst[pl.ds(pl.multiple_of((2 * kk + 1 - c) * t, t), t), :] = sib[pl.ds(blk, t), :]


def stacked(ref, blk, t):
    rows = ref[pl.ds(blk, t), :]
    return jnp.concatenate([rows[:, i * HEAD : (i + 1) * HEAD] for i in range(GROUP)], axis=0)


def masked_scores(place, q, keys, segk, segq, kk, t):
    length = 2 * t * (kk + 1)
    s = dot_cols(q, keys[:length, :]) * SCALE
    mine = segq[kk * t : (kk + 1) * t, :]
    col = lax.broadcasted_iota(jnp.int32, (t, length), 1)
    row = lax.broadcasted_iota(jnp.int32, (t, length), 0) + (2 * kk + place[1]) * t
    same = jnp.concatenate([mine] * (length // HEAD), axis=1) == segk[:, :length]
    ok = same & (col <= row)
    ok = jnp.concatenate([ok.astype(F32)] * GROUP, axis=0) > 0.5
    return jnp.where(ok, s, -1e30)


def attend_body(reps, t, place, q, ko, vo, ks, vs, segk, segq, out, keys, values):
    fill(place, ko, ks, keys, reps, t)
    fill(place, vo, vs, values, reps, t)
    for kk in range(reps):
        blk = pl.multiple_of((kk ^ place[0]) * t, t)
        length = 2 * t * (kk + 1)
        s = masked_scores(place, stacked(q, blk, t), keys, segk, segq, kk, t)
        p = jnp.exp(s - jnp.max(s, axis=-1, keepdims=True))
        p = p * (1.0 / jnp.sum(p, axis=-1, keepdims=True))
        o = dot(p.astype(BF), values[:length, :])
        for i in range(GROUP):
            out[pl.ds(blk, t), i * HEAD : (i + 1) * HEAD] = o[i * t : (i + 1) * t, :].astype(BF)


def head_specs(n, nk):
    wide = pl.BlockSpec((n, GROUP * HEAD), lambda g, _: (0, g))
    key = pl.BlockSpec((n, HEAD), lambda g, _: (0, g))
    value = pl.BlockSpec((n, HEAD), lambda g, _: (0, nk + g))
    return wide, key, value


def attend_call(place, q, kv, kv_sib, segk, segq, reps, nk):
    n = q.shape[0]
    t = n // reps
    wide, key, value = head_specs(n, nk)
    return pl.pallas_call(
        partial(attend_body, reps, t),
        out_shape=jax.ShapeDtypeStruct(q.shape, BF),
        grid_spec=pltpu.PrefetchScalarGridSpec(
            num_scalar_prefetch=1,
            grid=(nk,),
            in_specs=[wide, key, value, key, value, whole(*segk.shape), whole(*segq.shape)],
            out_specs=wide,
            scratch_shapes=[pltpu.VMEM((2 * n, HEAD), BF)] * 2,
        ),
        compiler_params=pltpu.CompilerParams(vmem_limit_bytes=VMEM_LIMIT),
        cost_estimate=pl.CostEstimate(
            flops=4 * n * 2 * n * HEAD * nk * GROUP, transcendentals=2 * n * n * nk, bytes_accessed=4 << 20
        ),
        name="attend",
    )(place, q, kv, kv, kv_sib, kv_sib, segk, segq)


def attend_back_body(
    reps, t, place, q, ko, vo, ks, vs, do, segk, segq, dq, dko, dvo, dks, dvs, keys, values, dkeys, dvalues
):
    fill(place, ko, ks, keys, reps, t)
    fill(place, vo, vs, values, reps, t)
    for kk in reversed(range(reps)):
        blk = pl.multiple_of((kk ^ place[0]) * t, t)
        length = 2 * t * (kk + 1)
        qs = stacked(q, blk, t)
        dos = stacked(do, blk, t)
        s = masked_scores(place, qs, keys, segk, segq, kk, t)
        p = jnp.exp(s - jnp.max(s, axis=-1, keepdims=True))
        p = p * (1.0 / jnp.sum(p, axis=-1, keepdims=True))
        dp = dot_cols(dos, values[:length, :])
        delta = jnp.sum(p * dp, axis=-1, keepdims=True)
        ds = (p * (dp - delta)).astype(BF)
        o = dot(ds, keys[:length, :]) * SCALE
        for i in range(GROUP):
            dq[pl.ds(blk, t), i * HEAD : (i + 1) * HEAD] = o[i * t : (i + 1) * t, :]
        dk = dot_rows(ds, qs) * SCALE
        dv = dot_rows(p.astype(BF), dos)
        if kk == reps - 1:
            dkeys[...] = dk
            dvalues[...] = dv
        else:
            dkeys[:length, :] += dk
            dvalues[:length, :] += dv
    r, c = place[0], place[1]
    for kk in range(reps):
        blk = pl.multiple_of((kk ^ r) * t, t)
        mine = pl.ds(pl.multiple_of((2 * kk + c) * t, t), t)
        theirs = pl.ds(pl.multiple_of((2 * kk + 1 - c) * t, t), t)
        dko[pl.ds(blk, t), :] = dkeys[mine, :]
        dvo[pl.ds(blk, t), :] = dvalues[mine, :]
        dks[pl.ds(blk, t), :] = dkeys[theirs, :].astype(BF)
        dvs[pl.ds(blk, t), :] = dvalues[theirs, :].astype(BF)


def attend_back_call(place, q, kv, kv_sib, do, segk, segq, reps, nk):
    n = q.shape[0]
    t = n // reps
    wide, key, value = head_specs(n, nk)
    narrow = jax.ShapeDtypeStruct((n, nk * HEAD), F32)
    narrow_b = jax.ShapeDtypeStruct((n, nk * HEAD), BF)
    return pl.pallas_call(
        partial(attend_back_body, reps, t),
        out_shape=(jax.ShapeDtypeStruct(q.shape, F32), narrow, narrow, narrow_b, narrow_b),
        grid_spec=pltpu.PrefetchScalarGridSpec(
            num_scalar_prefetch=1,
            grid=(nk,),
            in_specs=[wide, key, value, key, value, wide, whole(*segk.shape), whole(*segq.shape)],
            out_specs=(wide, key, key, key, key),
            scratch_shapes=[pltpu.VMEM((2 * n, HEAD), BF)] * 2 + [pltpu.VMEM((2 * n, HEAD), F32)] * 2,
        ),
        compiler_params=pltpu.CompilerParams(vmem_limit_bytes=VMEM_LIMIT),
        cost_estimate=pl.CostEstimate(
            flops=10 * n * 2 * n * HEAD * nk * GROUP, transcendentals=2 * n * n * nk, bytes_accessed=8 << 20
        ),
        name="attend_back",
    )(place, q, kv, kv, kv_sib, kv_sib, do, segk, segq)


def head_back_body(nq, nk, dq, dko, dvo, dks, dvs, proj, cs, sn, qg, kg, out, dqg, dkg):
    @pl.when(pl.program_id(0) == 0)
    def _():
        dqg[...] = jnp.zeros_like(dqg)
        dkg[...] = jnp.zeros_like(dkg)

    cosine, sine = cs[...], sn[...]
    for n in range(nq + nk):
        at = slice(n * HEAD, (n + 1) * HEAD)
        if n < nq:
            d, gain, total = dq[:, at], qg[...], dqg
        else:
            part = slice((n - nq) * HEAD, (n - nq + 1) * HEAD)
            d, gain, total = dko[:, part] + dks[:, part].astype(F32), kg[...], dkg
        dy = rotate_back(d, cosine, sine)
        v = proj[:, at]
        rs = lax.rsqrt(jnp.mean(v * v, axis=-1, keepdims=True) + EPS)
        hat = v * rs
        gdy = dy * gain
        dv = rs * (gdy - hat * jnp.mean(hat * gdy, axis=-1, keepdims=True))
        out[:, at] = dv.astype(BF)
        total[...] += jnp.sum(dy * hat, axis=0, keepdims=True)
    first = (nq + nk) * HEAD
    out[:, first:] = (dvo[...] + dvs[...].astype(F32)).astype(BF)


def head_back_call(dq, dko, dvo, dks, dvs, proj, cs, sn, qg, kg, reps, nq, nk):
    n = dq.shape[0]
    t = n // reps
    rows = lambda width: pl.BlockSpec((t, width), lambda i: (i, 0))
    gain = jax.ShapeDtypeStruct((1, HEAD), F32)
    return pl.pallas_call(
        partial(head_back_body, nq, nk),
        out_shape=(jax.ShapeDtypeStruct((n, (nq + 2 * nk) * HEAD), BF), gain, gain),
        grid=(reps,),
        in_specs=[
            rows(nq * HEAD),
            *[rows(nk * HEAD)] * 4,
            rows((nq + nk) * HEAD),
            rows(HEAD),
            rows(HEAD),
            whole(1, HEAD),
            whole(1, HEAD),
        ],
        out_specs=(rows((nq + 2 * nk) * HEAD), whole(1, HEAD), whole(1, HEAD)),
        compiler_params=pltpu.CompilerParams(vmem_limit_bytes=VMEM_LIMIT),
        cost_estimate=pl.CostEstimate(flops=n * nq * HEAD * 40, transcendentals=0, bytes_accessed=8 << 20),
        name="head_back",
    )(dq, dko, dvo, dks, dvs, proj, cs, sn, qg, kg)


def rms(x):
    return lax.rsqrt(jnp.mean(x * x, axis=-1, keepdims=True) + EPS)


def rms_back(x, gain, dy):
    rs = rms(x)
    gdy = dy * gain
    return rs * gdy - x * (rs * rs * rs) * jnp.mean(x * gdy, axis=-1, keepdims=True)


def local(reps, ctxs, tokens, segment_ids, positions, cotangent, qkv_weight, out_weight, attn_gain, query_gain,
          key_gain, mlp_gain, gate_up_weight, down_weight):
    move = Moves(reps, ctxs)
    line = ctxs // 2
    layers, d_rows, qkv_cols = qkv_weight.shape
    width = tokens.shape[2]
    t = tokens.shape[1]
    n = reps * t
    ff = gate_up_weight.shape[2] // 2
    ffr = ff // reps
    nq, nk = QUERY_HEADS // reps, KEY_VALUE_HEADS // reps
    out_rows, down_rows = out_weight.shape[1] // reps, down_weight.shape[1] // reps
    r = lax.axis_index("rep")
    core = lax.axis_index("ctx") % 2
    place = jnp.stack([r, core]).astype(jnp.int32)

    x = move.turn(tokens[0])
    marks = move.turn(jnp.concatenate([segment_ids, positions], axis=0))
    top = move.turn(cotangent[0])
    gains = lax.all_gather(
        jnp.concatenate([attn_gain, mlp_gain, query_gain, key_gain], axis=1), "ctx", axis=0
    ).astype(F32)
    at = 0
    gain_sets = []
    for size in (d_rows, d_rows, HEAD // ctxs, HEAD // ctxs):
        part = gains[:, :, at : at + size]
        gain_sets.append(part.transpose(1, 0, 2).reshape(layers, 1, ctxs * size))
        at += size
    gain_a, gain_m, gain_q, gain_k = gain_sets

    def columns(l):
        sl = lambda w, start, size: lax.dynamic_slice(w, (0, start + r * size), (d_rows, size))
        w, gu = qkv_weight[l], gate_up_weight[l]
        qkv = jnp.concatenate(
            [
                sl(w, 0, nq * HEAD),
                sl(w, QUERY_HEADS * HEAD, nk * HEAD),
                sl(w, (QUERY_HEADS + KEY_VALUE_HEADS) * HEAD, nk * HEAD),
            ],
            axis=1,
        )
        gate_up = jnp.concatenate([sl(gu, 0, ffr), sl(gu, ff, ffr)], axis=1)
        return qkv, gate_up

    def rows(l):
        piece = jnp.concatenate(
            [
                lax.dynamic_slice(out_weight[l], (r * out_rows, 0), (out_rows, width)),
                lax.dynamic_slice(down_weight[l], (r * down_rows, 0), (down_rows, width)),
            ],
            axis=0,
        )
        return move.turn(piece)

    def by_core(piece):
        size = piece.shape[1]
        return piece.reshape(line, 2, size, width).transpose(1, 0, 2, 3).reshape(ctxs * size, width)

    def by_place(value):
        size = value.shape[0] // ctxs
        return value.reshape(2, line, size, width).transpose(1, 0, 2, 3).reshape(ctxs, size, width)

    weights = []
    row_pieces = [rows(l) for l in range(layers)]
    for l in range(layers):
        qkv, gate_up = columns(l)
        w_qkv = lax.all_gather(qkv, "ctx", axis=0, tiled=True)
        w_rows = lax.all_gather(row_pieces[l], "ctx", axis=0)
        w_gu = lax.all_gather(gate_up, "ctx", axis=0, tiled=True)
        weights.append((w_qkv, by_core(w_rows[:, :out_rows]), w_gu, by_core(w_rows[:, out_rows:])))

    seg_all, pos_all = marks[0], marks[1]
    slice_of = lambda v, k: lax.dynamic_slice(v, ((2 * k + core) * t,), (t,))
    pos_mine = jnp.concatenate([slice_of(pos_all, j ^ r) for j in range(reps)])
    seg_mine = jnp.concatenate([slice_of(seg_all, k) for k in range(reps)])
    segk = seg_all[None, :]
    segq = jnp.broadcast_to(seg_mine[:, None], (n, HEAD))
    frequency = THETA ** (-(jnp.arange(HEAD // 2).astype(F32) * 2.0) / HEAD)
    angle = pos_mine.astype(F32)[:, None] * frequency[None, :]
    cosine, sine = jnp.cos(angle), jnp.sin(angle)
    cs = jnp.concatenate([cosine, cosine], axis=1)
    sn = jnp.concatenate([-sine, sine], axis=1)

    x = x.astype(F32)
    saved = []
    for l in range(layers):
        w_qkv, w_out, w_gu, w_down = weights[l]
        normed = move.gather((x * rms(x) * gain_a[l]).astype(BF))
        q, kv, proj = qkv_call(normed, w_qkv, gain_q[l], gain_k[l], cs, sn, nq, nk)
        kv_sib = move.sibling(kv)
        attended = attend_call(place, q, kv, kv_sib, segk, segq, reps, nk)
        middle = x + move.scatter(lambda d: dot(attended[d * t : (d + 1) * t], w_out))
        normed_mid = jnp.concatenate(move.gather((middle * rms(middle) * gain_m[l]).astype(BF)), axis=0)
        gate_up = dot(normed_mid, w_gu)
        hidden = (jax.nn.silu(gate_up[:, :ffr]) * gate_up[:, ffr:]).astype(BF)
        saved.append((x, normed, q, kv, kv_sib, proj, attended, middle, normed_mid, gate_up, hidden))
        x = middle + move.scatter(lambda d: dot(hidden[d * t : (d + 1) * t], w_down))
    outputs = move.turn(x.astype(BF))

    g = top.astype(F32)
    branch = top
    grads = [None] * layers
    for l in reversed(range(layers)):
        w_qkv, w_out, w_gu, w_down = weights[l]
        x, normed, q, kv, kv_sib, proj, attended, middle, normed_mid, gate_up, hidden = saved[l]
        branch = jnp.concatenate(move.gather(branch), axis=0)
        d_hidden = dot_cols(branch, w_down)
        gate, up = gate_up[:, :ffr], gate_up[:, ffr:]
        sig = jax.nn.sigmoid(gate)
        d_gate_up = jnp.concatenate(
            [
                (d_hidden * up * sig * (1.0 + gate * (1.0 - sig))).astype(BF),
                (d_hidden * (gate * sig)).astype(BF),
            ],
            axis=1,
        )
        d_normed_mid = move.scatter(lambda d: dot_cols(d_gate_up[d * t : (d + 1) * t], w_gu))
        d_middle = g + rms_back(middle, gain_m[l], d_normed_mid)
        out_branch = jnp.concatenate(move.gather(d_middle.astype(BF)), axis=0)
        down_g = dot_rows(hidden, branch).astype(BF)
        gu_g = dot_rows(normed_mid, d_gate_up).astype(BF)
        gu_g = lax.psum_scatter(gu_g, "ctx", scatter_dimension=0, tiled=True)
        d_attended = dot_cols(out_branch, w_out).astype(BF)
        dq, dko, dvo, dks, dvs = attend_back_call(place, q, kv, kv_sib, d_attended, segk, segq, reps, nk)
        dkv_sib = move.sibling(jnp.concatenate([dks, dvs], axis=1))
        out_g = dot_rows(attended, out_branch).astype(BF)
        row_g = jnp.concatenate([by_place(out_g), by_place(down_g)], axis=1)
        row_g = lax.psum_scatter(row_g, "ctx", scatter_dimension=0, tiled=False)
        d_proj, dqg, dkg = head_back_call(
            dq, dko, dvo, dkv_sib[:, : nk * HEAD], dkv_sib[:, nk * HEAD :], proj, cs, sn, gain_q[l], gain_k[l],
            reps, nq, nk,
        )
        d_normed = move.scatter(lambda d: dot_cols(d_proj[d * t : (d + 1) * t], w_qkv))
        qkv_g = dot_rows(jnp.concatenate(normed, axis=0), d_proj).astype(BF)
        qkv_g = lax.psum_scatter(qkv_g, "ctx", scatter_dimension=0, tiled=True)
        g = d_middle + rms_back(x, gain_a[l], d_normed)
        branch = g.astype(BF)
        grads[l] = (qkv_g, gu_g, row_g, dqg, dkg)
    input_grad = move.turn(branch).astype(F32)

    head_gains = jnp.concatenate([jnp.concatenate(grads[l][3:], axis=0) for l in range(layers)], axis=0)
    head_gains = lax.psum(head_gains, AXES).reshape(layers, 2, ctxs, HEAD // ctxs)
    head_gains = lax.dynamic_index_in_dim(head_gains, lax.axis_index("ctx"), axis=2, keepdims=False)

    full = []
    for l in range(layers):
        qkv_g, gu_g, row_g, _, _ = grads[l]
        row_g = move.turn(row_g)
        parts = [move.gather(v) for v in (qkv_g, gu_g, row_g)]

        def ordered(pieces, cut):
            stack = jnp.stack([cut(p) for p in pieces])
            return [lax.dynamic_index_in_dim(stack, k ^ r, axis=0, keepdims=False) for k in range(reps)]

        def across(pieces, cuts):
            return jnp.concatenate(
                [p for lo, hi in cuts for p in ordered(pieces, lambda v: v[:, lo:hi])], axis=1
            ).astype(F32)

        a, b = nq * HEAD, (nq + nk) * HEAD
        qkv_full = across(parts[0], ((0, a), (a, b), (b, b + nk * HEAD)))
        gu_full = across(parts[1], ((0, ffr), (ffr, 2 * ffr)))
        out_full = jnp.concatenate(ordered(parts[2], lambda v: v[:out_rows]), axis=0).astype(F32)
        down_full = jnp.concatenate(ordered(parts[2], lambda v: v[out_rows:]), axis=0).astype(F32)
        attn_g = jnp.sum(qkv_weight[l].astype(F32) * qkv_full, axis=1) / attn_gain[l].astype(F32)
        mlp_g = jnp.sum(gate_up_weight[l].astype(F32) * gu_full, axis=1) / mlp_gain[l].astype(F32)
        full.append((qkv_full, out_full, attn_g, head_gains[l, 0], head_gains[l, 1], mlp_g, gu_full, down_full))
    stacked_grads = [jnp.stack([full[l][i] for l in range(layers)]) for i in range(8)]
    return (outputs[None], input_grad[None], *stacked_grads)


def solution(mesh):
    return jax.shard_map(
        partial(local, mesh.shape["rep"], mesh.shape["ctx"]),
        mesh=mesh,
        in_specs=(
            P("rep", "ctx", None),
            P("rep", None),
            P("rep", None),
            P("rep", "ctx", None),
            P(None, "ctx", None),
            P(None, "ctx", None),
            P(None, "ctx"),
            P(None, "ctx"),
            P(None, "ctx"),
            P(None, "ctx"),
            P(None, "ctx", None),
            P(None, "ctx", None),
        ),
        out_specs=(
            P("rep", "ctx", None),
            P("rep", "ctx", None),
            P(None, "ctx", None),
            P(None, "ctx", None),
            P(None, "ctx"),
            P(None, "ctx"),
            P(None, "ctx"),
            P(None, "ctx"),
            P(None, "ctx", None),
            P(None, "ctx", None),
        ),
        check_vma=False,
    )
```

time: 2010 us -> 816 us (0.41)
  waiting for transfers between devices: 1400 us -> 183 us
  starting transfers between devices: 1.82 us -> 229 us
  matrix products: 298 us -> 74.5 us
  local copies, waits for them, and re-layouts: 127 us -> 65.1 us
  Pallas kernels: 0 us -> 59.6 us
  blocking collectives: 93.4 us -> 146 us
  other arithmetic: 53.5 us -> 32 us
    reduce_scatter x10 -> x6, waiting for transfers between devices: 717 us -> 0.03 us  [the longest x2 0.02 us: local(): qkv_g = lax.psum_scatter(qkv_g, 'ctx', scatter_dimension=0, tiled=True)]
    all_gather x12 -> x6, waiting for transfers between devices: 546 us -> 0.06 us  [the longest x2 0.02 us: local(): w_rows = lax.all_gather(row_pieces[l], 'ctx', axis=0)]
    ppermute x0 -> x79, starting transfers between devices: none -> 228 us  [the longest x42 154 us: gather(): pieces[d] = lax.ppermute(value, AXES, self.peer[d])]
    dot_general x136 -> x46, matrix products: 298 us -> 74.5 us  [the longest x20 34.6 us: dot_cols(): lax.dot_general(a, b, (((1,), (1,)), ((), ())), preferred_element_type=F32)]
    ppermute x0 -> x79, waiting for transfers between devices: none -> 183 us  [the longest x42 115 us: gather(): pieces[d] = lax.ppermute(value, AXES, self.peer[d])]
    psum x1 -> x0, waiting for transfers between devices: 115 us -> none  [local(): lax.psum(as_sent(flat), 'rep')]
    all_gather x4 -> x1, blocking collectives: 42.2 us -> 107 us  [local(): lax.all_gather(jnp.concatenate([attn_gain, mlp_gain, query_gain, key_gain...]
    pallas_call x0 -> x8, Pallas kernels: none -> 59.6 us  [the longest x2 20.4 us: attend_back_call(): pl.pallas_call(partial(attend_back_body, reps, t), out_shape=(jax.ShapeDt...]
  transfers between devices with their start and end apart: 25 -> 91, of which waited for: 22 -> 50; matrix products, arithmetic and copies ran while one was open for 11% -> 15% of each run, Pallas kernels for 0% -> 5%
where the time goes in v1:
time: 816 us; the launch traced here: 806 us
  starting transfers between devices  229 us (28%)
  waiting for transfers between devices  183 us (22%)
  blocking collectives  146 us (18%)
  matrix products  74.5 us (9%)
  local copies, waits for them, and re-layouts  65.1 us (8%)
  Pallas kernels  59.6 us (7%)
  other arithmetic  32 us (4%)
  between operations  17.4 us (2%)
    ppermute x42, starting transfers between devices, gather(): pieces[d] = lax.ppermute(value, AXES, self.peer[d])  154 us
    ppermute x42, waiting for transfers between devices, gather(): pieces[d] = lax.ppermute(value, AXES, self.peer[d])  115 us
    all_gather x1, blocking collectives, local(): lax.all_gather(jnp.concatenate([attn_gain, mlp_gain, query_gain, key_gain...  107 us
    ppermute x24, waiting for transfers between devices, scatter(): lax.ppermute(make(d).astype(BF), AXES, self.peer[d])  62.9 us
    ppermute x24, starting transfers between devices, scatter(): lax.ppermute(make(d).astype(BF), AXES, self.peer[d])  58.4 us
    psum x1, blocking collectives, local(): lax.psum(head_gains, AXES).reshape(layers, 2, ctxs, HEAD // ctxs)  39.3 us
    dot_general x20, matrix products, dot_cols(): lax.dot_general(a, b, (((1,), (1,)), ((), ())), preferred_element_type=F32)  34.6 us
    dot_general x8, matrix products, dot_rows(): lax.dot_general(a, b, (((0,), (0,)), ((), ())), preferred_element_type=F32)  23.4 us
  transfers between devices with their start and end apart: 91, of which 50 were waited for; matrix products, arithmetic and copies ran while one was open for 15% of the time, Pallas kernels for 5%

profile of v1, /device:TPU:0, one launch (start us, length us, event | category | flops | bytes accessed | tf_op | source)
XLA Modules:
  0.0 806.2 jit_solution(3210090242783153403)
XLA Ops:
  23.9 106.6 %all-gather.3 = bf16[8,2,288]{2,1,0:T(2,128)(2,1)S(1)} all-gather(bf16[1,2,288]{2,1,0:T(2,128)(2,1)S(1)} %maximum_bitcast_fusion), channel_id=2, replica_groups=mesh['rep'=4,'ctx'=8] {'ctx'}, dimensions={0}, use_global_device_ids=true | all-gather | bytes 10368 | tf_op jit(solution)/shard_map/all_gather | solution.py:331
  133.2 3.9 collective-permute-start.3
  140.5 3.9 collective-permute-done.3.refs_3_
  144.3 5.0 collective-permute-done.2.refs_2_
  150.2 6.3 qkv.2
  159.6 7.4 attend.2
  173.0 6.6 collective-permute-done.7
  179.6 3.9 collective-permute-done.8
  191.4 3.8 collective-permute-done.12
  195.2 4.8 collective-permute-done.11
  200.0 3.9 fusion.86
  209.9 6.6 collective-permute-done.13
  216.5 3.8 collective-permute-done.14
  226.6 5.4 collective-permute-done.18.refs_3_
  232.0 4.7 collective-permute-done.17.refs_2_
  238.1 6.2 qkv.3
  244.4 3.8 collective-permute-start.31
  249.7 7.5 attend.3
  258.5 4.2 collective-permute-start.21
  267.9 18.3 %collective-permute-start.33 = (bf16[128,1024]{1,0:T(8,128)(2,1)}, bf16[128,1024]{1,0:T(8,128)(2,1)S(1)}, u32[]{:S(2)}, u32[]{:S(2)}) collective-permute-start(bf16[128,1024]{1,0:T(8,128)(2,1)} %collective-permute-done.31), channel_id=1, source_target_pairs={{0,16},{1,17},{2,18},{3,19},{4,20},{5,21},{6,22},{7,23},{8,24},{9,... | collective-permute-start | bytes 786440 | tf_op jit(solution)/shard_map/ppermute | solution.py:54
  292.7 5.0 collective-permute-done.32
  302.4 5.0 collective-permute-done.25
  308.4 4.0 fusion.85
  312.5 3.9 multiply_convert_fusion.2
  325.4 3.9 collective-permute-done.36
  329.3 4.1 collective-permute-done.35
  340.3 6.6 collective-permute-done.40
  346.9 3.2 collective-permute-done.39
  353.1 10.3 %attend_back.2 = (f32[512,512]{1,0:T(8,128)}, f32[512,256]{1,0:T(8,128)}, f32[512,256]{1,0:T(8,128)}, bf16[512,256]{1,0:T(8,128)(2,1)}, bf16[512,256]{1,0:T(8,128)(2,1)}) custom-call(s32[2]{0:T(128)} %pad_add_fusion.2.place, bf16[512,512]{1,0:T(8,128)(2,1)} %get-tuple-element.34.q, bf16[512,512]{1,0:T(8,128)(2,1)} %get-tuple-element.35.ko.vo, ...), custom_call_target="tpu_custom_call" | custom-call | flops 2684354560 | bytes 8388608 | tf_op jit(solution)/shard_map/attend_back/pallas_call | solution.py:233
  367.3 5.9 head_back.2
  373.2 3.8 convolution_convert_fusion.2
  383.6 5.2 convolution_convert_fusion
  398.1 3.8 collective-permute-done.42
  401.9 4.5 collective-permute-done.43
  411.4 6.6 collective-permute-done.47
  418.1 4.5 collective-permute-done.46
  433.6 3.3 collective-permute-done.49
  436.9 4.7 collective-permute-done.48
  447.5 6.6 collective-permute-done.53
  454.1 3.5 collective-permute-done.52
  460.6 10.1 %attend_back.3 = (f32[512,512]{1,0:T(8,128)}, f32[512,256]{1,0:T(8,128)}, f32[512,256]{1,0:T(8,128)}, bf16[512,256]{1,0:T(8,128)(2,1)}, bf16[512,256]{1,0:T(8,128)(2,1)}) custom-call(s32[2]{0:T(128)} %pad_add_fusion.2.place, bf16[512,512]{1,0:T(8,128)(2,1)} %get-tuple-element.32.q, bf16[512,512]{1,0:T(8,128)(2,1)} %get-tuple-element.33.ko.vo, ...), custom_call_target="tpu_custom_call" | custom-call | flops 2684354560 | bytes 8388608 | tf_op jit(solution)/shard_map/attend_back/pallas_call | solution.py:233
  474.6 5.9 head_back.3
  480.6 3.9 convolution_convert_fusion.3
  497.5 6.6 collective-permute-done.27
  504.1 3.9 collective-permute-done.28
  512.0 3.3 convolution_convert_fusion.12
  515.3 19.3 %collective-permute-start.55 = (bf16[128,1024]{1,0:T(8,128)(2,1)}, bf16[128,1024]{1,0:T(8,128)(2,1)S(1)}, u32[]{:S(2)}, u32[]{:S(2)}) collective-permute-start(bf16[128,1024]{1,0:T(8,128)(2,1)} %convolution_convert_fusion.12), channel_id=1, source_target_pairs={{0,24},{1,25},{2,26},{3,27},{4,28},{5,29},{6,30},{7,31},{8,16},{9,... | collective-permute-start | bytes 786440 | tf_op jit(solution)/shard_map/ppermute | solution.py:58
  537.1 11.2 %collective-permute-start.56 = (bf16[128,1024]{1,0:T(8,128)(2,1)}, bf16[128,1024]{1,0:T(8,128)(2,1)S(1)}, u32[]{:S(2)}, u32[]{:S(2)}) collective-permute-start(bf16[128,1024]{1,0:T(8,128)(2,1)} %convolution_convert_fusion.11), channel_id=1, source_target_pairs={{0,8},{1,9},{2,10},{3,11},{4,12},{5,13},{6,14},{7,15},{8,0},{9,1},... | collective-permute-start | bytes 786440 | tf_op jit(solution)/shard_map/ppermute | solution.py:58
  552.2 4.6 convolution_convert_fusion.1
  557.5 39.3 %psum.7 = f32[2,2,8,16]{3,1,0,2:T(2,128)S(1)} all-reduce(f32[2,2,8,16]{3,1,0,2:T(2,128)S(1)} %copy.49), channel_id=1, replica_groups=mesh['rep'=4,'ctx'=8] {'rep','ctx'}, use_global_device_ids=true, to_apply=%region_14.15 | all-reduce | flops 512 | bytes 4096 | tf_op jit(solution)/shard_map/psum | solution.py:453
  603.4 20.6 %collective-permute-start.64 = (bf16[128,1024]{1,0:T(8,128)(2,1)}, bf16[128,1024]{1,0:T(8,128)(2,1)S(1)}, u32[]{:S(2)}, u32[]{:S(2)}) collective-permute-start(bf16[128,1024]{1,0:T(8,128)(2,1)} %reduce-scatter.9.cloned.1.call-done), channel_id=1, source_target_pairs={{0,24},{1,25},{2,26},{3,27},{4,28},{5,29},{6,30},{7,31},{8,16},{9,... | collective-permute-start | bytes 786440 | tf_op jit(solution)/shard_map/ppermute | solution.py:54
  624.9 14.1 %collective-permute-start.63 = (bf16[128,1024]{1,0:T(8,128)(2,1)}, bf16[128,1024]{1,0:T(8,128)(2,1)S(1)}, u32[]{:S(2)}, u32[]{:S(2)}) collective-permute-start(bf16[128,1024]{1,0:T(8,128)(2,1)} %reduce-scatter.9.cloned.1.call-done), channel_id=1, source_target_pairs={{0,16},{1,17},{2,18},{3,19},{4,20},{5,21},{6,22},{7,23},{8,24},{9,... | collective-permute-start | bytes 786440 | tf_op jit(solution)/shard_map/ppermute | solution.py:54
  640.0 7.3 collective-permute-done.63
  651.6 15.6 %collective-permute-start.72 = (bf16[160,1024]{1,0:T(8,128)(2,1)S(1)}, bf16[160,1024]{1,0:T(8,128)(2,1)}, u32[]{:S(2)}, u32[]{:S(2)}) collective-permute-start(bf16[160,1024]{1,0:T(8,128)(2,1)S(1)} %collective-permute-done.69), channel_id=1, source_target_pairs={{0,24},{1,25},{2,26},{3,27},{4,28},{5,29},{6,30},{7,31},{8,16},{9,... | collective-permute-start | bytes 983048 | tf_op jit(solution)/shard_map/ppermute | solution.py:54
  667.2 13.4 %collective-permute-start.71 = (bf16[160,1024]{1,0:T(8,128)(2,1)S(1)}, bf16[160,1024]{1,0:T(8,128)(2,1)}, u32[]{:S(2)}, u32[]{:S(2)}) collective-permute-start(bf16[160,1024]{1,0:T(8,128)(2,1)S(1)} %collective-permute-done.69), channel_id=1, source_target_pairs={{0,16},{1,17},{2,18},{3,19},{4,20},{5,21},{6,22},{7,23},{8,24},{9,... | collective-permute-start | bytes 983048 | tf_op jit(solution)/shard_map/ppermute | solution.py:54
  685.2 5.5 collective-permute-start.76
  699.2 10.7 %collective-permute-done.77 = bf16[128,1536]{1,0:T(8,128)(2,1)S(1)} collective-permute-done((bf16[128,1536]{1,0:T(8,128)(2,1)}, bf16[128,1536]{1,0:T(8,128)(2,1)S(1)}, u32[]{:S(2)}, u32[]{:S(2)}) %collective-permute-start.77) | collective-permute-done | bytes 393248 | tf_op jit(solution)/shard_map/ppermute | solution.py:54
  717.2 4.6 collective-permute-done.61
  721.8 4.3 collective-permute-done.60
  732.3 4.1 collective-permute-start.65
  737.0 12.7 %collective-permute-start.68 = (bf16[160,1024]{1,0:T(8,128)(2,1)}, bf16[160,1024]{1,0:T(8,128)(2,1)}, u32[]{:S(2)}, u32[]{:S(2)}) collective-permute-start(bf16[160,1024]{1,0:T(8,128)(2,1)} %collective-permute-done.65), channel_id=1, source_target_pairs={{0,24},{1,25},{2,26},{3,27},{4,28},{5,29},{6,30},{7,31},{8,16},{9,... | collective-permute-start | bytes 983048 | tf_op jit(solution)/shard_map/ppermute | solution.py:54
  752.9 12.0 %collective-permute-start.67 = (bf16[160,1024]{1,0:T(8,128)(2,1)}, bf16[160,1024]{1,0:T(8,128)(2,1)}, u32[]{:S(2)}, u32[]{:S(2)}) collective-permute-start(bf16[160,1024]{1,0:T(8,128)(2,1)} %collective-permute-done.65), channel_id=1, source_target_pairs={{0,16},{1,17},{2,18},{3,19},{4,20},{5,21},{6,22},{7,23},{8,24},{9,... | collective-permute-start | bytes 983048 | tf_op jit(solution)/shard_map/ppermute | solution.py:54
  773.0 8.1 %collective-permute-done.67 = bf16[160,1024]{1,0:T(8,128)(2,1)} collective-permute-done((bf16[160,1024]{1,0:T(8,128)(2,1)}, bf16[160,1024]{1,0:T(8,128)(2,1)}, u32[]{:S(2)}, u32[]{:S(2)}) %collective-permute-start.67) | collective-permute-done | bytes 327712 | tf_op jit(solution)/shard_map/ppermute | solution.py:54
  795.1 3.1 maximum_convert_fusion
  (641 shorter events, 229.3 us)
Async XLA Ops:
  7.2 142.2 %all-gather.11.cloned.1.call-start = ((), (), s32[]{:S(2)}) async-start(), calls=%async_computation.6 | async-start | bytes 2359296 | tf_op jit(solution)/shard_map/all_gather | solution.py:378
  10.8 156.1 %all-gather.19.cloned.1.call-start = ((), (), s32[]{:S(2)}) async-start(), calls=%async_computation.16 | async-start | bytes 2949120 | tf_op jit(solution)/shard_map/all_gather | solution.py:379
  15.8 184.2 %all-gather.13.cloned.1.call-start = ((), (), s32[]{:S(2)}) async-start(), calls=%async_computation.7 | async-start | bytes 3538944 | tf_op jit(solution)/shard_map/all_gather | solution.py:380
  17.1 209.5 %all-gather.15.cloned.1.call-start = ((), (), s32[]{:S(2)}) async-start(), calls=%async_computation.8 | async-start | bytes 2359296 | tf_op jit(solution)/shard_map/all_gather | solution.py:378
  19.7 228.5 %all-gather.21.cloned.1.call-start = ((), (), s32[]{:S(2)}) async-start(), calls=%async_computation.17 | async-start | bytes 2949120 | tf_op jit(solution)/shard_map/all_gather | solution.py:379
  19.8 113.0 %collective-permute-start.4 = (s32[2,1024]{1,0:T(2,128)S(1)}, s32[2,1024]{1,0:T(2,128)S(1)}, u32[]{:S(2)}, u32[]{:S(2)}) collective-permute-start(s32[2,1024]{1,0:T(2,128)S(1)} %pad_add_fusion), channel_id=1, source_target_pairs={{0,0},{1,1},{2,8},{3,9},{4,16},{5,17},{6,24},{7,25},{8,2},{9,3},{1... | collective-permute-start | bytes 24584 | tf_op jit(solution)/shard_map/ppermute | solution.py:46
  20.4 112.4 %collective-permute-start = (bf16[128,1024]{1,0:T(8,128)(2,1)S(1)}, bf16[128,1024]{1,0:T(8,128)(2,1)S(1)}, u32[]{:S(2)}, u32[]{:S(2)}) collective-permute-start(bf16[128,1024]{1,0:T(8,128)(2,1)S(1)} %bitcast.417), channel_id=1, source_target_pairs={{0,0},{1,1},{2,8},{3,9},{4,16},{5,17},{6,24},{7,25},{8,2},{9,3},{1... | collective-permute-start | bytes 786440 | tf_op jit(solution)/shard_map/ppermute | solution.py:46
  23.1 107.5 %collective-permute-start.20 = (bf16[160,1024]{1,0:T(8,128)(2,1)S(1)}, bf16[160,1024]{1,0:T(8,128)(2,1)S(1)}, u32[]{:S(2)}, u32[]{:S(2)}) collective-permute-start(bf16[160,1024]{1,0:T(8,128)(2,1)S(1)} %pad_maximum_fusion.26), channel_id=1, source_target_pairs={{0,0},{1,1},{2,8},{3,9},{4,16},{5,17},{6,24},{7,25},{8,2},{9,3},{1... | collective-permute-start | bytes 983048 | tf_op jit(solution)/shard_map/ppermute | solution.py:46
  131.4 168.9 %all-gather.17.cloned.1.call-start = ((), (), s32[]{:S(2)}) async-start(), calls=%async_computation.9 | async-start | bytes 3538944 | tf_op jit(solution)/shard_map/all_gather | solution.py:380
  133.2 11.1 %collective-permute-start.3 = (bf16[128,1024]{1,0:T(8,128)(2,1)S(1)}, bf16[128,1024]{1,0:T(8,128)(2,1)S(1)}, u32[]{:S(2)}, u32[]{:S(2)}) collective-permute-start(bf16[128,1024]{1,0:T(8,128)(2,1)S(1)} %fusion.34.refs_0_), channel_id=1, source_target_pairs={{0,24},{1,25},{2,26},{3,27},{4,28},{5,29},{6,30},{7,31},{8,16},{9,... | collective-permute-start | bytes 786440 | tf_op jit(solution)/shard_map/ppermute | solution.py:54
  137.1 12.3 %collective-permute-start.2 = (bf16[128,1024]{1,0:T(8,128)(2,1)S(1)}, bf16[128,1024]{1,0:T(8,128)(2,1)S(1)}, u32[]{:S(2)}, u32[]{:S(2)}) collective-permute-start(bf16[128,1024]{1,0:T(8,128)(2,1)S(1)} %fusion.34.refs_0_), channel_id=1, source_target_pairs={{0,16},{1,17},{2,18},{3,19},{4,20},{5,21},{6,22},{7,23},{8,24},{9,... | collective-permute-start | bytes 786440 | tf_op jit(solution)/shard_map/ppermute | solution.py:54
  137.1 12.3 %collective-permute-start.1 = (bf16[128,1024]{1,0:T(8,128)(2,1)S(1)}, bf16[128,1024]{1,0:T(8,128)(2,1)S(1)}, u32[]{:S(2)}, u32[]{:S(2)}) collective-permute-start(bf16[128,1024]{1,0:T(8,128)(2,1)S(1)} %fusion.34.refs_0_), channel_id=1, source_target_pairs={{0,8},{1,9},{2,10},{3,11},{4,12},{5,13},{6,14},{7,15},{8,0},{9,1},... | collective-permute-start | bytes 786440 | tf_op jit(solution)/shard_map/ppermute | solution.py:54
  171.2 12.3 %collective-permute-start.8 = (bf16[128,1024]{1,0:T(8,128)(2,1)S(1)}, bf16[128,1024]{1,0:T(8,128)(2,1)S(1)}, u32[]{:S(2)}, u32[]{:S(2)}) collective-permute-start(bf16[128,1024]{1,0:T(8,128)(2,1)S(1)} %convolution_convert_fusion.32), channel_id=1, source_target_pairs={{0,8},{1,9},{2,10},{3,11},{4,12},{5,13},{6,14},{7,15},{8,0},{9,1},... | collective-permute-start | bytes 786440 | tf_op jit(solution)/shard_map/ppermute | solution.py:58
  171.4 13.0 %collective-permute-start.9 = (bf16[128,1024]{1,0:T(8,128)(2,1)S(1)}, bf16[128,1024]{1,0:T(8,128)(2,1)S(1)}, u32[]{:S(2)}, u32[]{:S(2)}) collective-permute-start(bf16[128,1024]{1,0:T(8,128)(2,1)S(1)} %convolution_convert_fusion.31), channel_id=1, source_target_pairs={{0,16},{1,17},{2,18},{3,19},{4,20},{5,21},{6,22},{7,23},{8,24},{9,... | collective-permute-start | bytes 786440 | tf_op jit(solution)/shard_map/ppermute | solution.py:58
  186.9 13.1 %collective-permute-start.11 = (bf16[128,1024]{1,0:T(8,128)(2,1)S(1)}, bf16[128,1024]{1,0:T(8,128)(2,1)}, u32[]{:S(2)}, u32[]{:S(2)}) collective-permute-start(bf16[128,1024]{1,0:T(8,128)(2,1)S(1)} %multiply_convert_fusion.8), channel_id=1, source_target_pairs={{0,16},{1,17},{2,18},{3,19},{4,20},{5,21},{6,22},{7,23},{8,24},{9,... | collective-permute-start | bytes 786440 | tf_op jit(solution)/shard_map/ppermute | solution.py:54
  188.3 11.7 %collective-permute-start.10 = (bf16[128,1024]{1,0:T(8,128)(2,1)S(1)}, bf16[128,1024]{1,0:T(8,128)(2,1)}, u32[]{:S(2)}, u32[]{:S(2)}) collective-permute-start(bf16[128,1024]{1,0:T(8,128)(2,1)S(1)} %multiply_convert_fusion.8), channel_id=1, source_target_pairs={{0,8},{1,9},{2,10},{3,11},{4,12},{5,13},{6,14},{7,15},{8,0},{9,1},... | collective-permute-start | bytes 786440 | tf_op jit(solution)/shard_map/ppermute | solution.py:54
  189.4 414.0 %reduce-scatter.9.cloned.1.call-start = ((), (), s32[]{:S(2)}) async-start(), calls=%async_computation.11 | async-start | bytes 2359296 | tf_op jit(solution)/shard_map/reduce_scatter | solution.py:446
  208.2 12.1 %collective-permute-start.14 = (bf16[128,1024]{1,0:T(8,128)(2,1)S(1)}, bf16[128,1024]{1,0:T(8,128)(2,1)S(1)}, u32[]{:S(2)}, u32[]{:S(2)}) collective-permute-start(bf16[128,1024]{1,0:T(8,128)(2,1)S(1)} %convolution_convert_fusion.29), channel_id=1, source_target_pairs={{0,8},{1,9},{2,10},{3,11},{4,12},{5,13},{6,14},{7,15},{8,0},{9,1},... | collective-permute-start | bytes 786440 | tf_op jit(solution)/shard_map/ppermute | solution.py:58
  208.4 12.7 %collective-permute-start.15 = (bf16[128,1024]{1,0:T(8,128)(2,1)S(1)}, bf16[128,1024]{1,0:T(8,128)(2,1)S(1)}, u32[]{:S(2)}, u32[]{:S(2)}) collective-permute-start(bf16[128,1024]{1,0:T(8,128)(2,1)S(1)} %convolution_convert_fusion.28), channel_id=1, source_target_pairs={{0,16},{1,17},{2,18},{3,19},{4,20},{5,21},{6,22},{7,23},{8,24},{9,... | collective-permute-start | bytes 786440 | tf_op jit(solution)/shard_map/ppermute | solution.py:58
  223.6 13.1 %collective-permute-start.17 = (bf16[128,1024]{1,0:T(8,128)(2,1)S(1)}, bf16[128,1024]{1,0:T(8,128)(2,1)S(1)}, u32[]{:S(2)}, u32[]{:S(2)}) collective-permute-start(bf16[128,1024]{1,0:T(8,128)(2,1)S(1)} %multiply_convert_fusion.7.refs_0_), channel_id=1, source_target_pairs={{0,16},{1,17},{2,18},{3,19},{4,20},{5,21},{6,22},{7,23},{8,24},{9,... | collective-permute-start | bytes 786440 | tf_op jit(solution)/shard_map/ppermute | solution.py:54
  224.2 12.5 %collective-permute-start.16 = (bf16[128,1024]{1,0:T(8,128)(2,1)S(1)}, bf16[128,1024]{1,0:T(8,128)(2,1)S(1)}, u32[]{:S(2)}, u32[]{:S(2)}) collective-permute-start(bf16[128,1024]{1,0:T(8,128)(2,1)S(1)} %multiply_convert_fusion.7.refs_0_), channel_id=1, source_target_pairs={{0,8},{1,9},{2,10},{3,11},{4,12},{5,13},{6,14},{7,15},{8,0},{9,1},... | collective-permute-start | bytes 786440 | tf_op jit(solution)/shard_map/ppermute | solution.py:54
  244.4 20.6 %collective-permute-start.31 = (bf16[128,1024]{1,0:T(8,128)(2,1)}, bf16[128,1024]{1,0:T(8,128)(2,1)}, u32[]{:S(2)}, u32[]{:S(2)}) collective-permute-start(bf16[128,1024]{1,0:T(8,128)(2,1)} %bitcast.49), channel_id=1, source_target_pairs={{0,0},{1,1},{2,8},{3,9},{4,16},{5,17},{6,24},{7,25},{8,2},{9,3},{1... | collective-permute-start | bytes 786440 | tf_op jit(solution)/shard_map/ppermute | solution.py:46
  258.5 29.3 %collective-permute-start.21 = (bf16[128,1024]{1,0:T(8,128)(2,1)S(1)}, bf16[128,1024]{1,0:T(8,128)(2,1)S(1)}, u32[]{:S(2)}, u32[]{:S(2)}) collective-permute-start(bf16[128,1024]{1,0:T(8,128)(2,1)S(1)} %convolution_convert_fusion.27), channel_id=1, source_target_pairs={{0,24},{1,25},{2,26},{3,27},{4,28},{5,29},{6,30},{7,31},{8,16},{9,... | collective-permute-start | bytes 786440 | tf_op jit(solution)/shard_map/ppermute | solution.py:58
  264.3 23.5 %collective-permute-start.22 = (bf16[128,1024]{1,0:T(8,128)(2,1)S(1)}, bf16[128,1024]{1,0:T(8,128)(2,1)S(1)}, u32[]{:S(2)}, u32[]{:S(2)}) collective-permute-start(bf16[128,1024]{1,0:T(8,128)(2,1)S(1)} %convolution_convert_fusion.26), channel_id=1, source_target_pairs={{0,8},{1,9},{2,10},{3,11},{4,12},{5,13},{6,14},{7,15},{8,0},{9,1},... | collective-permute-start | bytes 786440 | tf_op jit(solution)/shard_map/ppermute | solution.py:58
  264.4 23.5 %collective-permute-start.23 = (bf16[128,1024]{1,0:T(8,128)(2,1)S(1)}, bf16[128,1024]{1,0:T(8,128)(2,1)S(1)}, u32[]{:S(2)}, u32[]{:S(2)}) collective-permute-start(bf16[128,1024]{1,0:T(8,128)(2,1)S(1)} %convolution_convert_fusion.25), channel_id=1, source_target_pairs={{0,16},{1,17},{2,18},{3,19},{4,20},{5,21},{6,22},{7,23},{8,24},{9,... | collective-permute-start | bytes 786440 | tf_op jit(solution)/shard_map/ppermute | solution.py:58
  264.9 34.2 %collective-permute-start.34 = (bf16[128,1024]{1,0:T(8,128)(2,1)}, bf16[128,1024]{1,0:T(8,128)(2,1)S(1)}, u32[]{:S(2)}, u32[]{:S(2)}) collective-permute-start(bf16[128,1024]{1,0:T(8,128)(2,1)} %collective-permute-done.31), channel_id=1, source_target_pairs={{0,24},{1,25},{2,26},{3,27},{4,28},{5,29},{6,30},{7,31},{8,16},{9,... | collective-permute-start | bytes 786440 | tf_op jit(solution)/shard_map/ppermute | solution.py:54
  267.9 30.5 %collective-permute-start.33 = (bf16[128,1024]{1,0:T(8,128)(2,1)}, bf16[128,1024]{1,0:T(8,128)(2,1)S(1)}, u32[]{:S(2)}, u32[]{:S(2)}) collective-permute-start(bf16[128,1024]{1,0:T(8,128)(2,1)} %collective-permute-done.31), channel_id=1, source_target_pairs={{0,16},{1,17},{2,18},{3,19},{4,20},{5,21},{6,22},{7,23},{8,24},{9,... | collective-permute-start | bytes 786440 | tf_op jit(solution)/shard_map/ppermute | solution.py:54
  289.2 13.2 %collective-permute-start.26 = (bf16[128,1024]{1,0:T(8,128)(2,1)}, bf16[128,1024]{1,0:T(8,128)(2,1)}, u32[]{:S(2)}, u32[]{:S(2)}) collective-permute-start(bf16[128,1024]{1,0:T(8,128)(2,1)} %multiply_convert_fusion.6), channel_id=1, source_target_pairs={{0,24},{1,25},{2,26},{3,27},{4,28},{5,29},{6,30},{7,31},{8,16},{9,... | collective-permute-start | bytes 786440 | tf_op jit(solution)/shard_map/ppermute | solution.py:54
  290.7 16.6 %collective-permute-start.25 = (bf16[128,1024]{1,0:T(8,128)(2,1)}, bf16[128,1024]{1,0:T(8,128)(2,1)}, u32[]{:S(2)}, u32[]{:S(2)}) collective-permute-start(bf16[128,1024]{1,0:T(8,128)(2,1)} %multiply_convert_fusion.6), channel_id=1, source_target_pairs={{0,16},{1,17},{2,18},{3,19},{4,20},{5,21},{6,22},{7,23},{8,24},{9,... | collective-permute-start | bytes 786440 | tf_op jit(solution)/shard_map/ppermute | solution.py:54
  297.7 10.8 %collective-permute-start.24 = (bf16[128,1024]{1,0:T(8,128)(2,1)}, bf16[128,1024]{1,0:T(8,128)(2,1)}, u32[]{:S(2)}, u32[]{:S(2)}) collective-permute-start(bf16[128,1024]{1,0:T(8,128)(2,1)} %multiply_convert_fusion.6), channel_id=1, source_target_pairs={{0,8},{1,9},{2,10},{3,11},{4,12},{5,13},{6,14},{7,15},{8,0},{9,1},... | collective-permute-start | bytes 786440 | tf_op jit(solution)/shard_map/ppermute | solution.py:54
  323.1 10.3 %collective-permute-start.35 = (bf16[128,1024]{1,0:T(8,128)(2,1)S(1)}, bf16[128,1024]{1,0:T(8,128)(2,1)S(1)}, u32[]{:S(2)}, u32[]{:S(2)}) collective-permute-start(bf16[128,1024]{1,0:T(8,128)(2,1)S(1)} %convolution_convert_fusion.21), channel_id=1, source_target_pairs={{0,24},{1,25},{2,26},{3,27},{4,28},{5,29},{6,30},{7,31},{8,16},{9,... | collective-permute-start | bytes 786440 | tf_op jit(solution)/shard_map/ppermute | solution.py:58
  339.0 11.1 %collective-permute-start.39 = (bf16[128,1024]{1,0:T(8,128)(2,1)S(1)}, bf16[128,1024]{1,0:T(8,128)(2,1)S(1)}, u32[]{:S(2)}, u32[]{:S(2)}) collective-permute-start(bf16[128,1024]{1,0:T(8,128)(2,1)S(1)} %get-tuple-element.66), channel_id=1, source_target_pairs={{0,16},{1,17},{2,18},{3,19},{4,20},{5,21},{6,22},{7,23},{8,24},{9,... | collective-permute-start | bytes 786440 | tf_op jit(solution)/shard_map/ppermute | solution.py:54
  339.5 11.2 %collective-permute-start.38 = (bf16[128,1024]{1,0:T(8,128)(2,1)S(1)}, bf16[128,1024]{1,0:T(8,128)(2,1)S(1)}, u32[]{:S(2)}, u32[]{:S(2)}) collective-permute-start(bf16[128,1024]{1,0:T(8,128)(2,1)S(1)} %get-tuple-element.66), channel_id=1, source_target_pairs={{0,8},{1,9},{2,10},{3,11},{4,12},{5,13},{6,14},{7,15},{8,0},{9,1},... | collective-permute-start | bytes 786440 | tf_op jit(solution)/shard_map/ppermute | solution.py:54
  377.1 272.8 %reduce-scatter.13.cloned.1.call-start = ((), (), s32[]{:S(2)}) async-start(), calls=%async_computation.13 | async-start | bytes 2949120 | tf_op jit(solution)/shard_map/reduce_scatter | solution.py:439
  383.5 297.1 %reduce-scatter.17.cloned.1.call-start = ((), (), s32[]{:S(2)}) async-start(), calls=%async_computation.15 | async-start | bytes 3538944 | tf_op jit(solution)/shard_map/reduce_scatter | solution.py:433
  388.8 322.8 %reduce-scatter.7.cloned.1.call-start = ((), (), s32[]{:S(2)}) async-start(), calls=%async_computation.10 | async-start | bytes 2359296 | tf_op jit(solution)/shard_map/reduce_scatter | solution.py:446
  395.4 11.0 %collective-permute-start.43 = (bf16[128,1024]{1,0:T(8,128)(2,1)S(1)}, bf16[128,1024]{1,0:T(8,128)(2,1)S(1)}, u32[]{:S(2)}, u32[]{:S(2)}) collective-permute-start(bf16[128,1024]{1,0:T(8,128)(2,1)S(1)} %convolution_convert_fusion.17), channel_id=1, source_target_pairs={{0,8},{1,9},{2,10},{3,11},{4,12},{5,13},{6,14},{7,15},{8,0},{9,1},... | collective-permute-start | bytes 786440 | tf_op jit(solution)/shard_map/ppermute | solution.py:58
  409.7 12.9 %collective-permute-start.46 = (bf16[128,1024]{1,0:T(8,128)(2,1)S(1)}, bf16[128,1024]{1,0:T(8,128)(2,1)S(1)}, u32[]{:S(2)}, u32[]{:S(2)}) collective-permute-start(bf16[128,1024]{1,0:T(8,128)(2,1)S(1)} %get-tuple-element.64), channel_id=1, source_target_pairs={{0,16},{1,17},{2,18},{3,19},{4,20},{5,21},{6,22},{7,23},{8,24},{9,... | collective-permute-start | bytes 786440 | tf_op jit(solution)/shard_map/ppermute | solution.py:54
  410.3 12.2 %collective-permute-start.45 = (bf16[128,1024]{1,0:T(8,128)(2,1)S(1)}, bf16[128,1024]{1,0:T(8,128)(2,1)S(1)}, u32[]{:S(2)}, u32[]{:S(2)}) collective-permute-start(bf16[128,1024]{1,0:T(8,128)(2,1)S(1)} %get-tuple-element.64), channel_id=1, source_target_pairs={{0,8},{1,9},{2,10},{3,11},{4,12},{5,13},{6,14},{7,15},{8,0},{9,1},... | collective-permute-start | bytes 786440 | tf_op jit(solution)/shard_map/ppermute | solution.py:54
  430.0 11.6 %collective-permute-start.48 = (bf16[128,1024]{1,0:T(8,128)(2,1)S(1)}, bf16[128,1024]{1,0:T(8,128)(2,1)S(1)}, u32[]{:S(2)}, u32[]{:S(2)}) collective-permute-start(bf16[128,1024]{1,0:T(8,128)(2,1)S(1)} %convolution_convert_fusion.15), channel_id=1, source_target_pairs={{0,24},{1,25},{2,26},{3,27},{4,28},{5,29},{6,30},{7,31},{8,16},{9,... | collective-permute-start | bytes 786440 | tf_op jit(solution)/shard_map/ppermute | solution.py:58
  445.5 12.1 %collective-permute-start.52 = (bf16[128,1024]{1,0:T(8,128)(2,1)S(1)}, bf16[128,1024]{1,0:T(8,128)(2,1)S(1)}, u32[]{:S(2)}, u32[]{:S(2)}) collective-permute-start(bf16[128,1024]{1,0:T(8,128)(2,1)S(1)} %get-tuple-element.62), channel_id=1, source_target_pairs={{0,16},{1,17},{2,18},{3,19},{4,20},{5,21},{6,22},{7,23},{8,24},{9,... | collective-permute-start | bytes 786440 | tf_op jit(solution)/shard_map/ppermute | solution.py:54
  446.3 11.3 %collective-permute-start.51 = (bf16[128,1024]{1,0:T(8,128)(2,1)S(1)}, bf16[128,1024]{1,0:T(8,128)(2,1)S(1)}, u32[]{:S(2)}, u32[]{:S(2)}) collective-permute-start(bf16[128,1024]{1,0:T(8,128)(2,1)S(1)} %get-tuple-element.62), channel_id=1, source_target_pairs={{0,8},{1,9},{2,10},{3,11},{4,12},{5,13},{6,14},{7,15},{8,0},{9,1},... | collective-permute-start | bytes 786440 | tf_op jit(solution)/shard_map/ppermute | solution.py:54
  484.5 247.8 %reduce-scatter.11.cloned.1.call-start = ((), (), s32[]{:S(2)}) async-start(), calls=%async_computation.12 | async-start | bytes 2949120 | tf_op jit(solution)/shard_map/reduce_scatter | solution.py:439
  491.6 273.2 %reduce-scatter.15.cloned.1.call-start = ((), (), s32[]{:S(2)}) async-start(), calls=%async_computation.14 | async-start | bytes 3538944 | tf_op jit(solution)/shard_map/reduce_scatter | solution.py:433
  495.3 12.8 %collective-permute-start.28 = (bf16[128,1024]{1,0:T(8,128)(2,1)S(1)}, bf16[128,1024]{1,0:T(8,128)(2,1)S(1)}, u32[]{:S(2)}, u32[]{:S(2)}) collective-permute-start(bf16[128,1024]{1,0:T(8,128)(2,1)S(1)} %convolution_convert_fusion.23), channel_id=1, source_target_pairs={{0,8},{1,9},{2,10},{3,11},{4,12},{5,13},{6,14},{7,15},{8,0},{9,1},... | collective-permute-start | bytes 786440 | tf_op jit(solution)/shard_map/ppermute | solution.py:58
  496.1 12.7 %collective-permute-start.29 = (bf16[128,1024]{1,0:T(8,128)(2,1)S(1)}, bf16[128,1024]{1,0:T(8,128)(2,1)S(1)}, u32[]{:S(2)}, u32[]{:S(2)}) collective-permute-start(bf16[128,1024]{1,0:T(8,128)(2,1)S(1)} %convolution_convert_fusion.22), channel_id=1, source_target_pairs={{0,16},{1,17},{2,18},{3,19},{4,20},{5,21},{6,22},{7,23},{8,24},{9,... | collective-permute-start | bytes 786440 | tf_op jit(solution)/shard_map/ppermute | solution.py:58
  515.3 81.5 %collective-permute-start.55 = (bf16[128,1024]{1,0:T(8,128)(2,1)}, bf16[128,1024]{1,0:T(8,128)(2,1)S(1)}, u32[]{:S(2)}, u32[]{:S(2)}) collective-permute-start(bf16[128,1024]{1,0:T(8,128)(2,1)} %convolution_convert_fusion.12), channel_id=1, source_target_pairs={{0,24},{1,25},{2,26},{3,27},{4,28},{5,29},{6,30},{7,31},{8,16},{9,... | collective-permute-start | bytes 786440 | tf_op jit(solution)/shard_map/ppermute | solution.py:58
  537.1 59.7 %collective-permute-start.56 = (bf16[128,1024]{1,0:T(8,128)(2,1)}, bf16[128,1024]{1,0:T(8,128)(2,1)S(1)}, u32[]{:S(2)}, u32[]{:S(2)}) collective-permute-start(bf16[128,1024]{1,0:T(8,128)(2,1)} %convolution_convert_fusion.11), channel_id=1, source_target_pairs={{0,8},{1,9},{2,10},{3,11},{4,12},{5,13},{6,14},{7,15},{8,0},{9,1},... | collective-permute-start | bytes 786440 | tf_op jit(solution)/shard_map/ppermute | solution.py:58
  550.8 47.4 %collective-permute-start.57 = (bf16[128,1024]{1,0:T(8,128)(2,1)}, bf16[128,1024]{1,0:T(8,128)(2,1)}, u32[]{:S(2)}, u32[]{:S(2)}) collective-permute-start(bf16[128,1024]{1,0:T(8,128)(2,1)} %convolution_convert_fusion.10), channel_id=1, source_target_pairs={{0,16},{1,17},{2,18},{3,19},{4,20},{5,21},{6,22},{7,23},{8,24},{9,... | collective-permute-start | bytes 786440 | tf_op jit(solution)/shard_map/ppermute | solution.py:58
  603.4 36.6 %collective-permute-start.64 = (bf16[128,1024]{1,0:T(8,128)(2,1)}, bf16[128,1024]{1,0:T(8,128)(2,1)S(1)}, u32[]{:S(2)}, u32[]{:S(2)}) collective-permute-start(bf16[128,1024]{1,0:T(8,128)(2,1)} %reduce-scatter.9.cloned.1.call-done), channel_id=1, source_target_pairs={{0,24},{1,25},{2,26},{3,27},{4,28},{5,29},{6,30},{7,31},{8,16},{9,... | collective-permute-start | bytes 786440 | tf_op jit(solution)/shard_map/ppermute | solution.py:54
  624.9 22.4 %collective-permute-start.63 = (bf16[128,1024]{1,0:T(8,128)(2,1)}, bf16[128,1024]{1,0:T(8,128)(2,1)S(1)}, u32[]{:S(2)}, u32[]{:S(2)}) collective-permute-start(bf16[128,1024]{1,0:T(8,128)(2,1)} %reduce-scatter.9.cloned.1.call-done), channel_id=1, source_target_pairs={{0,16},{1,17},{2,18},{3,19},{4,20},{5,21},{6,22},{7,23},{8,24},{9,... | collective-permute-start | bytes 786440 | tf_op jit(solution)/shard_map/ppermute | solution.py:54
  651.6 33.6 %collective-permute-start.72 = (bf16[160,1024]{1,0:T(8,128)(2,1)S(1)}, bf16[160,1024]{1,0:T(8,128)(2,1)}, u32[]{:S(2)}, u32[]{:S(2)}) collective-permute-start(bf16[160,1024]{1,0:T(8,128)(2,1)S(1)} %collective-permute-done.69), channel_id=1, source_target_pairs={{0,24},{1,25},{2,26},{3,27},{4,28},{5,29},{6,30},{7,31},{8,16},{9,... | collective-permute-start | bytes 983048 | tf_op jit(solution)/shard_map/ppermute | solution.py:54
  667.2 26.2 %collective-permute-start.71 = (bf16[160,1024]{1,0:T(8,128)(2,1)S(1)}, bf16[160,1024]{1,0:T(8,128)(2,1)}, u32[]{:S(2)}, u32[]{:S(2)}) collective-permute-start(bf16[160,1024]{1,0:T(8,128)(2,1)S(1)} %collective-permute-done.69), channel_id=1, source_target_pairs={{0,16},{1,17},{2,18},{3,19},{4,20},{5,21},{6,22},{7,23},{8,24},{9,... | collective-permute-start | bytes 983048 | tf_op jit(solution)/shard_map/ppermute | solution.py:54
  680.6 14.7 %collective-permute-start.70 = (bf16[160,1024]{1,0:T(8,128)(2,1)S(1)}, bf16[160,1024]{1,0:T(8,128)(2,1)S(1)}, u32[]{:S(2)}, u32[]{:S(2)}) collective-permute-start(bf16[160,1024]{1,0:T(8,128)(2,1)S(1)} %collective-permute-done.69), channel_id=1, source_target_pairs={{0,8},{1,9},{2,10},{3,11},{4,12},{5,13},{6,14},{7,15},{8,0},{9,1},... | collective-permute-start | bytes 983048 | tf_op jit(solution)/shard_map/ppermute | solution.py:54
  680.6 18.6 %collective-permute-start.78 = (bf16[128,1536]{1,0:T(8,128)(2,1)}, bf16[128,1536]{1,0:T(8,128)(2,1)S(1)}, u32[]{:S(2)}, u32[]{:S(2)}) collective-permute-start(bf16[128,1536]{1,0:T(8,128)(2,1)} %reduce-scatter.17.cloned.1.call-done), channel_id=1, source_target_pairs={{0,24},{1,25},{2,26},{3,27},{4,28},{5,29},{6,30},{7,31},{8,16},{9,... | collective-permute-start | bytes 1179656 | tf_op jit(solution)/shard_map/ppermute | solution.py:54
  682.1 27.7 %collective-permute-start.77 = (bf16[128,1536]{1,0:T(8,128)(2,1)}, bf16[128,1536]{1,0:T(8,128)(2,1)S(1)}, u32[]{:S(2)}, u32[]{:S(2)}) collective-permute-start(bf16[128,1536]{1,0:T(8,128)(2,1)} %reduce-scatter.17.cloned.1.call-done), channel_id=1, source_target_pairs={{0,16},{1,17},{2,18},{3,19},{4,20},{5,21},{6,22},{7,23},{8,24},{9,... | collective-permute-start | bytes 1179656 | tf_op jit(solution)/shard_map/ppermute | solution.py:54
  685.2 25.7 %collective-permute-start.76 = (bf16[128,1536]{1,0:T(8,128)(2,1)}, bf16[128,1536]{1,0:T(8,128)(2,1)S(1)}, u32[]{:S(2)}, u32[]{:S(2)}) collective-permute-start(bf16[128,1536]{1,0:T(8,128)(2,1)} %reduce-scatter.17.cloned.1.call-done), channel_id=1, source_target_pairs={{0,8},{1,9},{2,10},{3,11},{4,12},{5,13},{6,14},{7,15},{8,0},{9,1},... | collective-permute-start | bytes 1179656 | tf_op jit(solution)/shard_map/ppermute | solution.py:54
  715.3 10.7 %collective-permute-start.60 = (bf16[128,1024]{1,0:T(8,128)(2,1)}, bf16[128,1024]{1,0:T(8,128)(2,1)S(1)}, u32[]{:S(2)}, u32[]{:S(2)}) collective-permute-start(bf16[128,1024]{1,0:T(8,128)(2,1)} %reduce-scatter.7.cloned.1.call-done), channel_id=1, source_target_pairs={{0,16},{1,17},{2,18},{3,19},{4,20},{5,21},{6,22},{7,23},{8,24},{9,... | collective-permute-start | bytes 786440 | tf_op jit(solution)/shard_map/ppermute | solution.py:54
  737.0 32.5 %collective-permute-start.68 = (bf16[160,1024]{1,0:T(8,128)(2,1)}, bf16[160,1024]{1,0:T(8,128)(2,1)}, u32[]{:S(2)}, u32[]{:S(2)}) collective-permute-start(bf16[160,1024]{1,0:T(8,128)(2,1)} %collective-permute-done.65), channel_id=1, source_target_pairs={{0,24},{1,25},{2,26},{3,27},{4,28},{5,29},{6,30},{7,31},{8,16},{9,... | collective-permute-start | bytes 983048 | tf_op jit(solution)/shard_map/ppermute | solution.py:54
  752.9 28.2 %collective-permute-start.67 = (bf16[160,1024]{1,0:T(8,128)(2,1)}, bf16[160,1024]{1,0:T(8,128)(2,1)}, u32[]{:S(2)}, u32[]{:S(2)}) collective-permute-start(bf16[160,1024]{1,0:T(8,128)(2,1)} %collective-permute-done.65), channel_id=1, source_target_pairs={{0,16},{1,17},{2,18},{3,19},{4,20},{5,21},{6,22},{7,23},{8,24},{9,... | collective-permute-start | bytes 983048 | tf_op jit(solution)/shard_map/ppermute | solution.py:54
  764.9 17.1 %collective-permute-start.66 = (bf16[160,1024]{1,0:T(8,128)(2,1)}, bf16[160,1024]{1,0:T(8,128)(2,1)}, u32[]{:S(2)}, u32[]{:S(2)}) collective-permute-start(bf16[160,1024]{1,0:T(8,128)(2,1)} %collective-permute-done.65), channel_id=1, source_target_pairs={{0,8},{1,9},{2,10},{3,11},{4,12},{5,13},{6,14},{7,15},{8,0},{9,1},... | collective-permute-start | bytes 983048 | tf_op jit(solution)/shard_map/ppermute | solution.py:54
  766.0 23.6 %collective-permute-start.75 = (bf16[128,1536]{1,0:T(8,128)(2,1)}, bf16[128,1536]{1,0:T(8,128)(2,1)S(1)}, u32[]{:S(2)}, u32[]{:S(2)}) collective-permute-start(bf16[128,1536]{1,0:T(8,128)(2,1)} %reduce-scatter.15.cloned.1.call-done), channel_id=1, source_target_pairs={{0,24},{1,25},{2,26},{3,27},{4,28},{5,29},{6,30},{7,31},{8,16},{9,... | collective-permute-start | bytes 1179656 | tf_op jit(solution)/shard_map/ppermute | solution.py:54
  767.5 22.8 %collective-permute-start.74 = (bf16[128,1536]{1,0:T(8,128)(2,1)}, bf16[128,1536]{1,0:T(8,128)(2,1)S(1)}, u32[]{:S(2)}, u32[]{:S(2)}) collective-permute-start(bf16[128,1536]{1,0:T(8,128)(2,1)} %reduce-scatter.15.cloned.1.call-done), channel_id=1, source_target_pairs={{0,16},{1,17},{2,18},{3,19},{4,20},{5,21},{6,22},{7,23},{8,24},{9,... | collective-permute-start | bytes 1179656 | tf_op jit(solution)/shard_map/ppermute | solution.py:54
  769.5 21.8 %collective-permute-start.73 = (bf16[128,1536]{1,0:T(8,128)(2,1)}, bf16[128,1536]{1,0:T(8,128)(2,1)S(1)}, u32[]{:S(2)}, u32[]{:S(2)}) collective-permute-start(bf16[128,1536]{1,0:T(8,128)(2,1)} %reduce-scatter.15.cloned.1.call-done), channel_id=1, source_target_pairs={{0,8},{1,9},{2,10},{3,11},{4,12},{5,13},{6,14},{7,15},{8,0},{9,1},... | collective-permute-start | bytes 1179656 | tf_op jit(solution)/shard_map/ppermute | solution.py:54
  (136 other events, 1248.7 us)
Sparse Core Ops, SparseCore 0:
  11.0 75.2 all-gather.10
  88.4 40.3 all-gather.18
  131.0 37.3 all-gather.12
  170.5 28.0 all-gather.14
  200.1 33.0 all-gather.20
  234.7 53.1 all-gather.16
  377.2 35.4 reduce-scatter.8
  415.5 36.4 reduce-scatter.12
  454.9 39.4 reduce-scatter.16
  496.5 46.1 reduce-scatter.6
  545.1 39.3 reduce-scatter.10
  587.2 55.1 reduce-scatter.14
